TPU v7x, 32 devices: a whole 2x2x4 slice. The times are simulated.
32 devices in a mesh: slab: 8 (over z, x), pen: 4 (over y, core).
Axes of the slice: x: 2, y: 2, z: 4, core: 2. Of those that a mesh axis runs over, the one named last changes fastest.
Arguments:
- charges: bfloat16 [1024, 128], P(('slab', 'pen')), may hold values from -6 to 6
- counts: int32 [1024], P(('slab', 'pen')), may hold values from 32 to 128
- proj_weight: bfloat16 [1024, 128, 128], P(('slab', 'pen')), may hold values from -0.5 to 0.5
- dest_slab: int32 [1024, 1], P(('slab', 'pen')), may hold values from 0 to 3; in each aligned block of 32 rows (0 to 31, 32 to 63, ...) at most 16 rows name the same one
- box_index: int32 [1024], P(('slab', 'pen')), may hold values from 0 to 8191
- pair_target: int32 [2048], P(('slab', 'pen')), may hold values from 0 to 31
- pair_source: int32 [2048], P(('slab', 'pen')), may hold values from 0 to 31
- near_matrix: bfloat16 [2048, 128, 128], P(('slab', 'pen')), may hold values from -0.5 to 0.5
- kernel_hat: float32 [2, 256, 256, 512], P(None, None, 'slab', 'pen'), may hold values from -8 to 8, as said below
Outputs:
- potential: bfloat16 [1024, 128], P(('slab', 'pen'))
Inputs may be any that keep to these rules, and one draw needn't show every extreme that they name: `dest_slab`: each block's box lies in the lower half of the depth; among the 32 blocks of one device no slab is named more than 16 times. `pair_target`: local indices of blocks held by the same device as the pair. `pair_source`: local indices of blocks held by the same device as the pair. Hermitian, as the transform of a real kernel: with indices taken modulo 256, 256 and 512, kernel_hat[0] at (-u, -v, -w) equals kernel_hat[0] at (u, v, w), and kernel_hat[1] at (-u, -v, -w) equals minus kernel_hat[1] at (u, v, w).
All inputs are finite; a program needn't handle non-finite values.
Results may differ from a plain program's by a relative error of at most 0.0039.
Values may be sent and summed in bfloat16 or wider, within the bound.
No kernel may reach another device: no remote copies, remote signals or barrier semaphores. Data moves between devices by JAX's collectives and lax.ppermute only.
A program may use at most 128 MiB of HBM per device.

v0:
```python
import math

import jax
import jax.numpy as jnp
from jax import lax
from jax.sharding import PartitionSpec as P

highest = lax.Precision.HIGHEST


def passed_along(block, axis, distance):
    devices = range(lax.axis_size(axis))
    route = [((i - distance) % len(devices), i) for i in devices]
    return lax.ppermute(block, axis, route)


def dft_tables(length, positions):
    freqs = jnp.arange(length, dtype=jnp.int32)
    phase = positions[:, None] * freqs[None, :] % length
    angle = phase.astype(jnp.float32) * (2.0 * math.pi / length)
    return (jnp.cos(angle), jnp.sin(angle))


def forward_axis(paired, cosine, sine, form):
    real_part = paired[0]
    imag_part = paired[1]
    new_real = jnp.einsum(form, real_part, cosine, precision=highest) + jnp.einsum(
        form, imag_part, sine, precision=highest
    )
    new_imag = jnp.einsum(form, imag_part, cosine, precision=highest) - jnp.einsum(
        form, real_part, sine, precision=highest
    )
    return jnp.stack([new_real, new_imag])


def inverse_axis(paired, cosine, sine, form):
    real_part = paired[0]
    imag_part = paired[1]
    new_real = jnp.einsum(form, real_part, cosine, precision=highest) - jnp.einsum(
        form, imag_part, sine, precision=highest
    )
    new_imag = jnp.einsum(form, imag_part, cosine, precision=highest) + jnp.einsum(
        form, real_part, sine, precision=highest
    )
    return jnp.stack([new_real, new_imag])


def stencil_cells(boxes, rows_pen, width_x):
    per_row = width_x // 8
    per_plane = rows_pen // 4 * per_row
    box_z = boxes // per_plane
    box_y = boxes // per_row % (rows_pen // 4)
    box_x = boxes % per_row
    offsets = jnp.arange(128, dtype=jnp.int32)
    depth_cell = 4 * box_z[..., None] + offsets // 32
    row_cell = 4 * box_y[..., None] + offsets // 8 % 4
    col_cell = 8 * box_x[..., None] + offsets % 8
    return (depth_cell * rows_pen + row_cell) * width_x + col_cell


def shards(
    charges,
    counts,
    proj_weight,
    dest_slab,
    box_index,
    pair_target,
    pair_source,
    near_matrix,
    kernel_hat,
):
    blocks, slots = charges.shape
    stencil = proj_weight.shape[2]
    slab_count = lax.axis_size("slab")
    pen_count = lax.axis_size("pen")
    depth = kernel_hat.shape[1]
    width_y = kernel_hat.shape[2] * slab_count
    width_x = kernel_hat.shape[3] * pen_count
    planes = depth // slab_count
    rows_pen = width_y // pen_count
    capacity = max(2, 4 * blocks // slab_count)
    total_blocks = blocks * slab_count * pen_count
    factor = 1.0 / math.sqrt(float(depth) * width_y * width_x * total_blocks * stencil)
    live = jnp.arange(slots, dtype=jnp.int32)[None, :] < counts[:, None]
    charge = jnp.where(live, charges, jnp.zeros_like(charges))
    spread = jnp.einsum("bp,bps->bs", charge, proj_weight, preferred_element_type=jnp.float32)
    target_slab = dest_slab[:, 0]
    onehot = (target_slab[:, None] == jnp.arange(slab_count, dtype=jnp.int32)[None, :]).astype(
        jnp.int32
    )
    earlier = jnp.cumsum(onehot, axis=0) - onehot
    rank = jnp.sum(earlier * onehot, axis=1)
    send_values = (
        jnp.zeros((slab_count, capacity, stencil), jnp.float32).at[target_slab, rank].set(spread)
    )
    send_boxes = jnp.zeros((slab_count, capacity), jnp.int32).at[target_slab, rank].set(box_index)
    recv_values, recv_boxes = (
        lax.all_to_all(send_values, "slab", split_axis=0, concat_axis=0, tiled=True),
        lax.all_to_all(send_boxes, "slab", split_axis=0, concat_axis=0, tiled=True),
    )
    cells = stencil_cells(recv_boxes, rows_pen, width_x)
    grid = jnp.zeros((planes * rows_pen * width_x,), jnp.float32)
    grid = (
        grid.at[cells.reshape(-1)].add(recv_values.reshape(-1)).reshape(planes, rows_pen, width_x)
    )
    half = planes // 2
    moved = passed_along(grid[half:], "slab", slab_count // 2)
    lower = lax.axis_index("slab") < slab_count // 2
    field = jnp.where(lower, grid[:half], moved)
    order = jnp.arange(depth // 2, dtype=jnp.int32)
    holder = order // half
    depth_rows = (
        holder % (slab_count // 2) * planes + holder // (slab_count // 2) * half + order % half
    )
    x_cos, x_sin = dft_tables(width_x, jnp.arange(width_x, dtype=jnp.int32))
    y_cos, y_sin = dft_tables(width_y, jnp.arange(width_y, dtype=jnp.int32))
    z_cos, z_sin = dft_tables(depth, depth_rows)
    spectrum = jnp.stack(
        [
            jnp.einsum("zyn,nk->zyk", field, x_cos, precision=highest),
            -jnp.einsum("zyn,nk->zyk", field, x_sin, precision=highest),
        ]
    )
    spectrum = forward_axis(
        lax.all_to_all(spectrum, "pen", split_axis=3, concat_axis=2, tiled=True),
        y_cos,
        y_sin,
        "zyx,yk->zkx",
    )
    columns = lax.all_to_all(spectrum, "slab", split_axis=2, concat_axis=1, tiled=True)
    transformed = forward_axis(columns, z_cos, z_sin, "zyx,zk->kyx")
    kernel_real = kernel_hat[0]
    kernel_imag = kernel_hat[1]
    product = jnp.stack(
        [
            kernel_real * transformed[0] - kernel_imag * transformed[1],
            kernel_real * transformed[1] + kernel_imag * transformed[0],
        ]
    )
    returned = inverse_axis(product, z_cos, z_sin, "kyx,zk->zyx")
    rows_done = inverse_axis(
        lax.all_to_all(returned, "slab", split_axis=1, concat_axis=2, tiled=True),
        y_cos,
        y_sin,
        "zkx,yk->zyx",
    )
    paired = lax.all_to_all(rows_done, "pen", split_axis=2, concat_axis=3, tiled=True)
    real_out = jnp.einsum("zyk,nk->zyn", paired[0], x_cos, precision=highest)
    real_out = real_out - jnp.einsum("zyk,nk->zyn", paired[1], x_sin, precision=highest)
    potential_grid = real_out * factor
    partner = passed_along(potential_grid.astype(jnp.bfloat16), "slab", slab_count // 2).astype(
        potential_grid.dtype
    )
    potential_grid = jnp.concatenate([potential_grid, partner], axis=0)
    samples = potential_grid.reshape(-1)[cells].astype(jnp.bfloat16)
    answered = lax.all_to_all(samples, "slab", split_axis=0, concat_axis=0, tiled=True)
    mine = answered[target_slab, rank]
    far = jnp.einsum("bps,bs->bp", proj_weight, mine, preferred_element_type=jnp.float32)
    driven = charge[pair_source]
    terms = jnp.einsum("tpq,tq->tp", near_matrix, driven, preferred_element_type=jnp.float32)
    owners = (pair_target[:, None] == jnp.arange(blocks, dtype=jnp.int32)[None, :]).astype(
        jnp.float32
    )
    near = jnp.einsum("tb,tp->bp", owners, terms, precision=highest)
    total = jnp.where(live, far + near, jnp.zeros_like(far))
    return total.astype(jnp.bfloat16)


def solution(mesh):
    placed = (
        P(("slab", "pen"), None),
        P(("slab", "pen")),
        P(("slab", "pen"), None, None),
        P(("slab", "pen"), None),
        P(("slab", "pen")),
        P(("slab", "pen")),
        P(("slab", "pen")),
        P(("slab", "pen"), None, None),
        P(None, None, "slab", "pen"),
    )
    return jax.shard_map(
        shards, mesh=mesh, in_specs=placed, out_specs=P(("slab", "pen"), None), check_vma=False
    )
```

profile of v0, /device:TPU:0, one launch (start us, length us, event | category | flops | bytes accessed | tf_op | source)
XLA Modules:
  0.0 1122.1 jit_solution(7987199966789598573)
XLA Ops:
  3.0 5.4 scatter_fusion
  8.4 7.3 all-to-all-start
  18.7 4.2 scatter_fusion.1
  22.9 6.0 all-to-all-start.1
  29.1 6.7 all-to-all-done.1
  35.8 111.2 %scatter_custom_fusion.2 = f32[1048576]{0:T(1024)} fusion(s32[16384]{0:T(1024)S(1)} %bitcast.197, f32[16384]{0:T(1024)S(1)} %bitcast.196, f32[]{:T(128)} %constant.193.clone.1), kind=kCustom, calls=%fused_computation.28 | custom fusion | flops 16384 | bytes 4194308 | tf_op jit(solution)/shard_map/scatter-add | solution.py:104
  146.9 4.5 fusion.186
  157.6 87.8 %collective-permute-done = f32[16,64,512]{2,1,0:T(8,128)} collective-permute-done((f32[16,64,512]{2,1,0:T(8,128)}, f32[16,64,512]{2,1,0:T(8,128)}, u32[]{:S(2)}, u32[]{:S(2)}) %collective-permute-start) | collective-permute-done | bytes 2097184 | tf_op jit(solution)/shard_map/ppermute | solution.py:14
  245.4 8.9 convolution_bitcast_fusion
  254.3 7.9 negate_bitcast_fusion
  264.7 9.1 copy.48
  273.8 8.6 reshape.427
  282.5 53.9 %all_to_all.82 = f32[4,1,262144]{2,1,0:T(1,128)} all-to-all(f32[4,1,262144]{2,1,0:T(1,128)} %reshape.427), channel_id=1, replica_groups=mesh['slab'=8,'pen'=4] {'pen'}, dimensions={0} | all-to-all | bytes 8388608 | tf_op jit(solution)/shard_map/all_to_all | solution.py:125
  336.8 15.2 %reduce = f32[4,262144]{1,0:T(4,128)} reduce(f32[4,1,262144]{2,1,0:T(1,128)} %all_to_all.82, f32[]{:T(128)} %broadcast.663), dimensions={1}, to_apply=%all_to_all.62.reduce_sub_computation | reduce | bytes 8388612 | tf_op jit(solution)/shard_map/all_to_all | solution.py:125
  352.0 9.3 reshape.428
  361.3 7.0 copy.49
  383.2 4.4 copy.54
  387.6 4.6 all-to-all-start.3
  392.2 7.7 fusion.181
  399.9 85.4 %all-to-all-done.3 = f32[2,16,256,128]{3,1,0,2:T(8,128)} async-done(((f32[2,16,256,128]{3,1,0,2:T(8,128)}), f32[2,16,256,128]{3,1,0,2:T(8,128)}, u32[]{:S(2)}, u32[]{:S(2)}) %all-to-all-start.3) | async-done | bytes 4194336 | tf_op jit(solution)/shard_map/all_to_all | solution.py:130
  488.5 4.0 fusion.48
  492.5 4.0 fusion.46
  496.5 4.2 convolution_add_fusion
  500.8 11.0 multiply_subtract_fusion
  526.8 96.7 %all_to_all.83 = f32[2,128,32,128]{3,2,0,1:T(8,128)S(1)} all-to-all(f32[2,128,32,128]{3,2,0,1:T(8,128)S(1)} %copy.61), channel_id=1, replica_groups=mesh['slab'=8,'pen'=4] {'slab'}, dimensions={1} | all-to-all | bytes 8388608 | tf_op jit(solution)/shard_map/all_to_all | solution.py:142
  639.6 50.7 %all_to_all.84 = f32[2,16,256,128]{3,1,0,2:T(8,128)S(1)} all-to-all(f32[2,16,256,128]{3,1,0,2:T(8,128)S(1)} %copy.63), channel_id=1, replica_groups=mesh['slab'=8,'pen'=4] {'pen'}, dimensions={2} | all-to-all | bytes 8388608 | tf_op jit(solution)/shard_map/all_to_all | solution.py:147
  698.4 10.0 fusion.9
  711.5 9.6 subtract_multiply_fusion
  723.1 46.0 %collective-permute-done.1 = bf16[16,64,512]{2,1,0:T(8,128)(2,1)} collective-permute-done((bf16[16,64,512]{2,1,0:T(8,128)(2,1)S(1)}, bf16[16,64,512]{2,1,0:T(8,128)(2,1)}, u32[]{:S(2)}, u32[]{:S(2)}) %collective-permute-start.1) | collective-permute-done | bytes 1048608 | tf_op jit(solution)/shard_map/ppermute | solution.py:14
  773.0 332.2 %gather_fusion = bf16[16384]{0:T(1024)(128)(2,1)} fusion(bf16[1048576]{0:T(1024)(128)(2,1)} %bitcast.168, s32[16384]{0:T(1024)S(1)} %broadcast_clamp_fusion), kind=kCustom, calls=%fused_computation | custom fusion | bytes 131072 | tf_op jit(solution)/shard_map/gather | solution.py:155
  1105.2 7.8 all-to-all-start.6
  1114.2 5.5 all-to-all-done.6
  (75 shorter events, 84.9 us)
Async XLA Ops:
  0.0 1113.0 %copy-start = (bf16[64,128,128]{2,1,0:T(8,128)(2,1)S(1)}, bf16[64,128,128]{2,1,0:T(8,128)(2,1)}, u32[]{:S(2)}) copy-start(bf16[64,128,128]{2,1,0:T(8,128)(2,1)} %param.16) | copy-start | bytes 6291460
  8.4 14.4 %all-to-all-start = ((s32[8,1,16]{2,1,0:T(1,128)}), s32[8,1,16]{2,1,0:T(1,128)S(1)}, u32[]{:S(2)}, u32[]{:S(2)}) async-start(s32[8,1,16]{2,1,0:T(1,128)} %bitcast.9), calls=%async_computation | async-start | bytes 8192 | tf_op jit(solution)/shard_map/all_to_all | solution.py:99
  22.9 12.9 %all-to-all-start.1 = ((f32[8,16,128]{2,1,0:T(8,128)}), f32[8,16,128]{2,1,0:T(8,128)S(1)}, u32[]{:S(2)}, u32[]{:S(2)}) async-start(f32[8,16,128]{2,1,0:T(8,128)} %scatter_fusion.1), calls=%async_computation.1 | async-start | bytes 131072 | tf_op jit(solution)/shard_map/all_to_all | solution.py:98
  154.2 91.2 %collective-permute-start = (f32[16,64,512]{2,1,0:T(8,128)}, f32[16,64,512]{2,1,0:T(8,128)}, u32[]{:S(2)}, u32[]{:S(2)}) collective-permute-start(f32[16,64,512]{2,1,0:T(8,128)} %slice.70), channel_id=1, source_target_pairs={{16,0},{20,4},{24,8},{28,12},{0,16},{4,20},{8,24},{12,28},{17,1},{... | collective-permute-start | bytes 6291464 | tf_op jit(solution)/shard_map/ppermute | solution.py:14
  157.6 96.7 %copy-start.3 = (f32[16,64,512]{2,1,0:T(8,128)S(1)}, f32[16,64,512]{2,1,0:T(8,128)}, u32[]{:S(2)}) copy-start(f32[16,64,512]{2,1,0:T(8,128)} %slice.68) | copy-start | bytes 6291460
  387.6 97.7 %all-to-all-start.3 = ((f32[2,16,256,128]{3,1,0,2:T(8,128)}), f32[2,16,256,128]{3,1,0,2:T(8,128)}, u32[]{:S(2)}, u32[]{:S(2)}) async-start(f32[2,16,256,128]{3,1,0,2:T(8,128)} %copy.54), calls=%async_computation.3 | async-start | bytes 8388608 | tf_op jit(solution)/shard_map/all_to_all | solution.py:130
  496.5 4.2 copy-start.1
  711.5 10.8 copy-start.6
  711.5 10.8 copy-start.4
  711.5 10.8 copy-start.5
  721.1 48.1 %collective-permute-start.1 = (bf16[16,64,512]{2,1,0:T(8,128)(2,1)S(1)}, bf16[16,64,512]{2,1,0:T(8,128)(2,1)}, u32[]{:S(2)}, u32[]{:S(2)}) collective-permute-start(bf16[16,64,512]{2,1,0:T(8,128)(2,1)S(1)} %subtract_multiply_fusion), channel_id=1, source_target_pairs={{16,0},{20,4},{24,8},{28,12},{0,16},{4,20},{8,24},{12,28},{17,1},{... | collective-permute-start | bytes 3145736 | tf_op jit(solution)/shard_map/ppermute | solution.py:14
  1105.2 15.2 %copy-start.2 = (bf16[32,128,128]{2,1,0:T(8,128)(2,1)S(1)}, bf16[32,128,128]{2,1,0:T(8,128)(2,1)}, u32[]{:S(2)}) copy-start(bf16[32,128,128]{2,1,0:T(8,128)(2,1)} %param.11) | copy-start | bytes 3145732
  1105.2 15.9 %copy-start.7 = (s32[64]{0:T(128)S(1)}, s32[64]{0:T(128)}, u32[]{:S(2)}) copy-start(s32[64]{0:T(128)} %param.14) | copy-start | bytes 772
  1105.2 14.5 %all-to-all-start.6 = ((bf16[8,16,128]{2,1,0:T(8,128)(2,1)}), bf16[8,16,128]{2,1,0:T(8,128)(2,1)S(1)}, u32[]{:S(2)}, u32[]{:S(2)}) async-start(bf16[8,16,128]{2,1,0:T(8,128)(2,1)} %bitcast.55), calls=%async_computation.6 | async-start | bytes 65536 | tf_op jit(solution)/shard_map/all_to_all | solution.py:156
where the time goes:
time: 1140 us; the launch traced here: 1120 us
  local copies, waits for them, and re-layouts  427 us (37%)
  waiting for transfers between devices  231 us (20%)
  blocking collectives  201 us (18%)
  other arithmetic  136 us (12%)
  matrix products  99 us (9%)
  starting transfers between devices  27.3 us (2%)
    gather x1, local copies, waits for them, and re-layouts, shards(): samples = potential_grid.reshape(-1)[cells].astype(jnp.bfloat16)  332 us
    ppermute x2, waiting for transfers between devices, passed_along(): return lax.ppermute(block, axis, route)  134 us
    scatter-add x1, other arithmetic, shards(): grid.at[cells.reshape(-1)].add(recv_values.reshape(-1))  111 us
    all_to_all x1, blocking collectives, shards(): lax.all_to_all(returned, 'slab', split_axis=1, concat_axis=2, tiled=True)  96.7 us
    all_to_all x1, waiting for transfers between devices, shards(): lax.all_to_all(spectrum, 'slab', split_axis=2, concat_axis=1, tiled=True)  85.4 us
    all_to_all x1, blocking collectives, shards(): lax.all_to_all(spectrum, 'pen', split_axis=3, concat_axis=2, tiled=True)  53.9 us
    all_to_all x1, blocking collectives, shards(): lax.all_to_all(rows_done, 'pen', split_axis=2, concat_axis=3, tiled=True)  50.7 us
  transfers between devices with their start and end apart: 6, of which 5 were waited for; matrix products, arithmetic and copies ran while one was open for 2% of the time, Pallas kernels for 0%

commit v1 on v0

v1 whole, which is shorter than its diff:
```python
import functools
import math

import jax
import jax.numpy as jnp
import ml_dtypes
import numpy as np
from jax import lax
from jax.experimental import pallas as pl
from jax.experimental.pallas import tpu as pltpu
from jax.sharding import PartitionSpec as P

AXES = ("slab", "pen")
CHUNK = 32
BOX_X = 8
LANES = CHUNK * BOX_X
TILE = 8
SLOTS = TILE * CHUNK
f32 = jnp.float32
bf16 = jnp.bfloat16


def halves(table):
    high = table.astype(ml_dtypes.bfloat16)
    low = (table - high.astype(np.float64)).astype(ml_dtypes.bfloat16)
    return high, low


def split(value):
    high = value.astype(bf16)
    return high, (value - high.astype(f32)).astype(bf16)


def dot(a, b):
    return jnp.dot(a, b, preferred_element_type=f32)


def dot_nt(a, b):
    return lax.dot_general(a, b, (((1,), (1,)), ((), ())), preferred_element_type=f32)


def dot_tn(a, b):
    return lax.dot_general(a, b, (((0,), (0,)), ((), ())), preferred_element_type=f32)


def dot3(a_high, a_low, b_high, b_low, mul=dot):
    return mul(a_high, b_high) + (mul(a_high, b_low) + mul(a_low, b_high))


def iota(shape, dim):
    return lax.broadcasted_iota(jnp.int32, shape, dim)


def ones_where(mask):
    return jnp.where(mask, 1.0, 0.0).astype(bf16)


def plan_kernel(z_boxes, meta_ref, rows_ref, sx_ref, yl_ref, xb_ref, cz_ref, pos_ref):
    blocks = rows_ref.shape[0]
    groups = blocks // 128
    tiles = sx_ref.shape[0] // TILE
    below = ones_where(iota((128, 128), 0) < iota((128, 128), 1))
    base = jnp.zeros((z_boxes, 128), f32)
    marks, before = [], []
    for g in range(groups):
        box_z = meta_ref[0:1, 128 * g : 128 * g + 128]
        mark = jnp.where(iota((z_boxes, 128), 0) == box_z.astype(jnp.int32), 1.0, 0.0)
        marks.append(mark)
        before.append(base + dot(mark.astype(bf16), below))
        base = base + jnp.sum(mark, axis=1, keepdims=True)
    used = (base.astype(jnp.int32) + (CHUNK - 1)) // CHUNK
    lower = ones_where(iota((z_boxes, z_boxes), 1) < iota((z_boxes, z_boxes), 0))
    start = dot(lower, used.astype(f32).astype(bf16))
    for g in range(groups):
        place = jnp.sum(marks[g] * (start * CHUNK + before[g]), axis=0, keepdims=True)
        pos_ref[0:1, 128 * g : 128 * g + 128] = place.astype(jnp.int32)
    end = start.astype(jnp.int32) + used
    for t in range(cz_ref.shape[1] // 128):
        lane = iota((z_boxes, 128), 1) + 128 * t
        passed = jnp.where(end <= lane, 1, 0)
        cz_ref[0:1, 128 * t : 128 * t + 128] = jnp.sum(passed, axis=0, keepdims=True)
    cz_ref[1:2, 0:128] = jnp.sum(used, axis=0, keepdims=True)
    keep = iota((128, LANES), 0) % BOX_X == iota((128, LANES), 1) % BOX_X

    def tile(t, carry):
        hot = ones_where(iota((SLOTS, blocks), 0) + SLOTS * t == pos_ref[0:1, :])
        ordered = dot(hot, rows_ref[...]).astype(bf16)
        meta = dot_nt(meta_ref[...].astype(bf16), hot)
        xb_ref[0:1, pl.ds(pl.multiple_of(SLOTS * t, SLOTS), SLOTS)] = meta[2:3].astype(jnp.int32)
        meta = meta.astype(bf16)
        for q in range(TILE):
            spread = ones_where(iota((SLOTS, LANES), 0) == CHUNK * q + iota((SLOTS, LANES), 1) // BOX_X)
            wide = jnp.where(keep, dot_tn(ordered, spread), 0.0)
            sx_ref[TILE * t + q] = jnp.sum(wide.reshape(16, BOX_X, LANES), axis=1)
            yl_ref[TILE * t + q] = dot(meta, spread)
        return carry

    lax.fori_loop(0, tiles, tile, 0)


def field_kernel(cz_ref, xb_ref, sx_ref, yl_ref, ty_ref, tx_ref, uh_ref, ul_ref, ih_ref, il_ref, kh_ref, out_ref, grid_ref, cols_ref, ex_ref):
    depth, cv, _ = grid_ref.shape
    nv = cv // 2
    nw = kh_ref.shape[3]
    freqs = kh_ref.shape[2]
    y_boxes = ty_ref.shape[1] // 2
    total = cz_ref[1, 0]

    def clear(z, carry):
        grid_ref[z] = jnp.zeros((cv, 2 * nw), f32)
        return carry

    lax.fori_loop(0, depth, clear, 0)

    def wipe(c, carry):
        out_ref[c] = jnp.zeros((16, LANES), f32)
        return carry

    lax.fori_loop(total, out_ref.shape[0], wipe, 0)

    def tables(c):
        for b in range(CHUNK):
            ex_ref[BOX_X * b : BOX_X * b + BOX_X, :] = tx_ref[xb_ref[0, CHUNK * c + b]]
        hot = ones_where(iota((y_boxes, LANES), 0) == yl_ref[c][1:2].astype(jnp.int32))
        along = dot(ty_ref[...], jnp.concatenate([hot, hot], axis=0))
        return split(ex_ref[...]), along

    def scatter(c, carry):
        (ex_high, ex_low), along = tables(c)
        box = sx_ref[c]
        parts = []
        for i in range(4):
            part = along[0:cv] * box[4 * i : 4 * i + 1]
            for j in range(1, 4):
                part = part + along[cv * j : cv * j + cv] * box[4 * i + j : 4 * i + j + 1]
            parts.append(part)
        high, low = split(jnp.concatenate(parts, axis=0))
        added = dot3(high, low, ex_high, ex_low).reshape(4, cv, 2 * nw)
        where = pl.ds(4 * cz_ref[0, c], 4)
        grid_ref[where] = grid_ref[where] + added
        return carry

    lax.fori_loop(0, total, scatter, 0)

    def to_columns(g, carry):
        rows = pl.ds(pl.multiple_of(8 * g, 8), 8)
        for z in range(depth // 8):
            piece = grid_ref[8 * z : 8 * z + 8, rows, :]
            cols_ref[rows, 8 * z : 8 * z + 8, :] = jnp.swapaxes(piece, 0, 1)
        return carry

    lax.fori_loop(0, cv // 8, to_columns, 0)

    def column(p, carry):
        real, imag = [], []
        for v in (2 * p, 2 * p + 1):
            re, im = cols_ref[v], cols_ref[nv + v]
            real.append(re[:, :nw] - im[:, nw:])
            imag.append(re[:, nw:] + im[:, :nw])
        field = jnp.concatenate([jnp.concatenate(real, axis=1), jnp.concatenate(imag, axis=1)], axis=0)
        high, low = split(field)
        spec = dot3(uh_ref[...], ul_ref[...], high, low)
        k_re = jnp.concatenate([kh_ref[2 * p, 0], kh_ref[2 * p + 1, 0]], axis=1)
        k_im = jnp.concatenate([kh_ref[2 * p, 1], kh_ref[2 * p + 1, 1]], axis=1)
        s_re, s_im = spec[:freqs], spec[freqs:]
        prod = jnp.concatenate([k_re * s_re - k_im * s_im, k_re * s_im + k_im * s_re], axis=0)
        high, low = split(prod)
        back = dot3(ih_ref[...], il_ref[...], high, low)
        for n in range(2):
            q_re = back[:depth, nw * n : nw * n + nw]
            q_im = back[depth:, nw * n : nw * n + nw]
            cols_ref[2 * p + n] = jnp.concatenate([q_re, q_im], axis=1)
            cols_ref[nv + 2 * p + n] = jnp.concatenate([q_im, -q_re], axis=1)
        return carry

    lax.fori_loop(0, nv // 2, column, 0)

    def to_planes(g, carry):
        rows = pl.ds(pl.multiple_of(8 * g, 8), 8)
        for z in range(depth // 8):
            piece = cols_ref[rows, 8 * z : 8 * z + 8, :]
            grid_ref[8 * z : 8 * z + 8, rows, :] = jnp.swapaxes(piece, 0, 1)
        return carry

    lax.fori_loop(0, cv // 8, to_planes, 0)

    def gather(c, carry):
        (ex_high, ex_low), along = tables(c)
        planes = grid_ref[pl.ds(4 * cz_ref[0, c], 4)].reshape(4 * cv, 2 * nw)
        high, low = split(planes)
        lines = dot3(high, low, ex_high, ex_low, dot_nt)
        rows = []
        for i in range(4):
            for j in range(4):
                rows.append(jnp.sum(along[cv * j : cv * j + cv] * lines[cv * i : cv * i + cv], axis=0, keepdims=True))
        out_ref[c] = jnp.concatenate(rows, axis=0)
        return carry

    lax.fori_loop(0, total, gather, 0)


def unsort_kernel(got_ref, pos_ref, out_ref, acc_ref):
    blocks = pos_ref.shape[1]
    tiles = got_ref.shape[0] // TILE
    keep = iota((128, LANES), 0) % BOX_X == iota((128, LANES), 1) % BOX_X
    repeat = ones_where(iota((128, 16), 0) // BOX_X == iota((128, 16), 1))
    acc_ref[...] = jnp.zeros_like(acc_ref)

    def tile(t, carry):
        rows = jnp.zeros((128, SLOTS), f32)
        for q in range(TILE):
            wide = jnp.where(keep, dot(repeat, got_ref[TILE * t + q].astype(bf16)), 0.0).astype(bf16)
            pick = ones_where(CHUNK * q + iota((LANES, SLOTS), 0) // BOX_X == iota((LANES, SLOTS), 1))
            rows = rows + dot(wide, pick)
        hot = ones_where(iota((SLOTS, blocks), 0) + SLOTS * t == pos_ref[0:1, :])
        acc_ref[...] += dot(rows.astype(bf16), hot)
        return carry

    lax.fori_loop(0, tiles, tile, 0)
    for g in range(blocks // 128):
        out_ref[128 * g : 128 * g + 128, :] = acc_ref[:, 128 * g : 128 * g + 128].T.astype(bf16)


def turn(length, steps):
    angle = 2.0 * math.pi * (steps % length) / length
    return np.cos(angle), np.sin(angle)


def shards(charges, counts, proj_weight, dest_slab, box_index, pair_target, pair_source, near_matrix, kernel_hat):
    blocks, slots = charges.shape
    stencil = proj_weight.shape[2]
    slab_count = lax.axis_size("slab")
    pen_count = lax.axis_size("pen")
    devices = slab_count * pen_count
    freqs, nv, nw = kernel_hat.shape[1:]
    depth = freqs // 2
    width_y = nv * slab_count
    width_x = nw * pen_count
    planes = freqs // slab_count
    rows_pen = width_y // pen_count
    total_blocks = blocks * devices
    z_boxes, y_boxes, x_boxes = depth // 4, width_y // 4, width_x // BOX_X
    chunks = -(-(total_blocks // CHUNK + z_boxes) // TILE) * TILE
    factor = 1.0 / math.sqrt(float(freqs) * width_y * width_x * total_blocks * stencil)
    slab, pen = lax.axis_index("slab"), lax.axis_index("pen")

    live = jnp.arange(slots, dtype=jnp.int32)[None, :] < counts[:, None]
    charge = jnp.where(live, charges, jnp.zeros_like(charges))
    spread = jnp.einsum("bp,bps->bs", charge, proj_weight, preferred_element_type=f32)

    per_plane = rows_pen // 4 * x_boxes
    box_z = dest_slab[:, 0] * (planes // 4) + box_index // per_plane
    box_y = pen * (rows_pen // 4) + box_index // x_boxes % (rows_pen // 4)
    box_x = box_index % x_boxes
    meta = jnp.stack([box_z, box_y, box_x]).astype(bf16)
    meta = jnp.pad(meta, ((0, 5), (0, stencil - blocks)))
    packet = jnp.concatenate([spread.astype(bf16), meta], axis=0)
    packets = lax.all_to_all(jnp.broadcast_to(packet, (devices,) + packet.shape), AXES, 0, 0, tiled=True)
    rows = packets[:, :blocks].reshape(total_blocks, stencil)
    boxes = packets[:, blocks:, :blocks].transpose(1, 0, 2).reshape(8, total_blocks).astype(f32)

    lane_tiles = -(-chunks // 128) * 128
    plan = pl.pallas_call(
        functools.partial(plan_kernel, z_boxes),
        out_shape=(
            jax.ShapeDtypeStruct((chunks, 16, LANES), f32),
            jax.ShapeDtypeStruct((chunks, 8, LANES), f32),
            jax.ShapeDtypeStruct((1, chunks * CHUNK), jnp.int32),
            jax.ShapeDtypeStruct((2, lane_tiles), jnp.int32),
            jax.ShapeDtypeStruct((1, total_blocks), jnp.int32),
        ),
        compiler_params=pltpu.CompilerParams(vmem_limit_bytes=48 << 20),
        name="plan",
    )
    sx, yl, xb, cz, pos = plan(boxes, rows)

    v_all, yb_all = np.arange(width_y), np.arange(y_boxes)
    cos, sin = turn(width_y, v_all[None, :, None] * (4 * yb_all[None, None, :] + np.arange(4)[:, None, None]))
    high, low = halves(np.stack([cos, -sin], axis=1))
    along = np.concatenate([high, low], axis=3)
    ty = lax.dynamic_slice_in_dim(jnp.asarray(along), slab * nv, nv, 2).reshape(8 * nv, 2 * y_boxes)

    x_all = jnp.arange(width_x, dtype=jnp.int32)[:, None]
    w_own = pen * nw + jnp.arange(nw, dtype=jnp.int32)[None, :]
    phase = (x_all * w_own % width_x).astype(f32) * (2.0 * math.pi / width_x)
    tx = jnp.concatenate([jnp.cos(phase), -jnp.sin(phase)], axis=1).reshape(x_boxes, BOX_X, 2 * nw)

    cos, sin = turn(freqs, np.arange(freqs)[:, None] * np.arange(depth)[None, :])
    forth = np.block([[cos, sin], [-sin, cos]])
    uh, ul = halves(forth)
    ih, il = halves(forth.T * factor)
    kh = jnp.transpose(kernel_hat, (2, 0, 1, 3))

    vmem = pl.BlockSpec(memory_space=pltpu.VMEM)
    smem = pl.BlockSpec(memory_space=pltpu.SMEM)
    field = pl.pallas_call(
        field_kernel,
        out_shape=jax.ShapeDtypeStruct((chunks, 16, LANES), f32),
        in_specs=[smem, smem] + [vmem] * 9,
        out_specs=vmem,
        scratch_shapes=[
            pltpu.VMEM((depth, 2 * nv, 2 * nw), f32),
            pltpu.VMEM((2 * nv, depth, 2 * nw), f32),
            pltpu.VMEM((LANES, 2 * nw), f32),
        ],
        compiler_params=pltpu.CompilerParams(vmem_limit_bytes=56 << 20),
        name="field",
    )
    got = field(cz, xb, sx, yl, ty, tx, jnp.asarray(uh), jnp.asarray(ul), jnp.asarray(ih), jnp.asarray(il), kh)
    unsort = pl.pallas_call(
        unsort_kernel,
        out_shape=jax.ShapeDtypeStruct((total_blocks, stencil), bf16),
        scratch_shapes=[pltpu.VMEM((stencil, total_blocks), f32)],
        compiler_params=pltpu.CompilerParams(vmem_limit_bytes=48 << 20),
        name="unsort",
    )
    partial = unsort(got, pos)
    shares = lax.all_to_all(partial.reshape(devices, blocks, stencil), AXES, 0, 0, tiled=True)
    samples = jnp.sum(shares.astype(f32), axis=0).astype(bf16)

    far = jnp.einsum("bps,bs->bp", proj_weight, samples, preferred_element_type=f32)
    driven = charge[pair_source]
    terms = jnp.einsum("tpq,tq->tp", near_matrix, driven, preferred_element_type=f32)
    owners = (pair_target[:, None] == jnp.arange(blocks, dtype=jnp.int32)[None, :]).astype(f32)
    near = jnp.einsum("tb,tp->bp", owners, terms, precision=lax.Precision.HIGHEST)
    total = jnp.where(live, far + near, jnp.zeros_like(far))
    return total.astype(bf16)


def solution(mesh):
    placed = (
        P(AXES, None),
        P(AXES),
        P(AXES, None, None),
        P(AXES, None),
        P(AXES),
        P(AXES),
        P(AXES),
        P(AXES, None, None),
        P(None, None, "slab", "pen"),
    )
    return jax.shard_map(shards, mesh=mesh, in_specs=placed, out_specs=P(AXES, None), check_vma=False)
```

time: 1140 us -> 129 us (0.11); the launches traced: 1120 us -> 129 us
  local copies, waits for them, and re-layouts: 427 us -> 18.7 us
  waiting for transfers between devices: 231 us -> 8.68 us
  blocking collectives: 201 us -> 0 us
  other arithmetic: 136 us -> 3.74 us
  matrix products: 99 us -> 4.3 us
  Pallas kernels: 0 us -> 80.3 us
  starting transfers between devices: 27.3 us -> 13.1 us
    gather x2 -> x0, local copies, waits for them, and re-layouts: 333 us -> none  [the longest x1 332 us: shards(): samples = potential_grid.reshape(-1)[cells].astype(jnp.bfloat16)]
    all_to_all x3 -> x0, blocking collectives: 201 us -> none  [the longest x1 96.7 us: shards(): lax.all_to_all(returned, 'slab', split_axis=1, concat_axis=2, tiled=True)]
    ppermute x2 -> x0, waiting for transfers between devices: 134 us -> none  [passed_along(): return lax.ppermute(block, axis, route)]
    scatter-add x1 -> x0, other arithmetic: 111 us -> none  [shards(): grid.at[cells.reshape(-1)].add(recv_values.reshape(-1))]
    dot_general x24 -> x4, matrix products: 99 us -> 4.3 us  [the longest x1 1.6 us: shards(): jnp.einsum('bp,bps->bs', charge, proj_weight, preferred_element_type=f32)]
    all_to_all x4 -> x2, waiting for transfers between devices: 97.6 us -> 8.68 us  [the longest x1 8.67 us: shards(): lax.all_to_all(partial.reshape(devices, blocks, stencil), AXES, 0, 0, til...]
    pallas_call x0 -> x3, Pallas kernels: none -> 80.3 us  [the longest x1 64.9 us: shards(): field(cz, xb, sx, yl, ty, tx, jnp.asarray(uh), jnp.asarray(ul), jnp.asarr...]
    slice x8 -> x1, local copies, waits for them, and re-layouts: 23.7 us -> 0.02 us  [shards(): rows = packets[:, :blocks].reshape(total_blocks, stencil)]
  transfers between devices with their start and end apart: 6 -> 2, of which waited for: 5 -> 1; matrix products, arithmetic and copies ran while one was open for 2% -> 13% of each run, Pallas kernels for 0% -> 0%
where the time goes in v1:
time: 129 us
  Pallas kernels  80.3 us (62%)
  local copies, waits for them, and re-layouts  18.7 us (14%)
  starting transfers between devices  13.1 us (10%)
  waiting for transfers between devices  8.68 us (7%)
  matrix products  4.3 us (3%)
  other arithmetic  3.74 us (3%)
    pallas_call x1, Pallas kernels, shards(): field(cz, xb, sx, yl, ty, tx, jnp.asarray(uh), jnp.asarray(ul), jnp.asarr...  64.9 us
    unnamed x23, local copies, waits for them, and re-layouts  15.7 us
    all_to_all x1, waiting for transfers between devices, shards(): lax.all_to_all(partial.reshape(devices, blocks, stencil), AXES, 0, 0, til...  8.67 us
    pallas_call x1, Pallas kernels, shards(): sx, yl, xb, cz, pos = plan(boxes, rows)  8.63 us
    all_to_all x1, starting transfers between devices, shards(): lax.all_to_all(jnp.broadcast_to(packet, (devices,) + packet.shape), AXES,...  7.3 us
    pallas_call x1, Pallas kernels, shards(): partial = unsort(got, pos)  6.8 us
    all_to_all x1, starting transfers between devices, shards(): lax.all_to_all(partial.reshape(devices, blocks, stencil), AXES, 0, 0, til...  5.83 us
  transfers between devices with their start and end apart: 2, of which 1 were waited for; matrix products, arithmetic and copies ran while one was open for 13% of the time, Pallas kernels for 0%

profile of v1, /device:TPU:0, one launch (start us, length us, event | category | flops | bytes accessed | tf_op | source)
XLA Modules:
  0.0 129.0 jit_solution(9736009347064672737)
XLA Ops:
  0.0 0.0 copy-start
  0.0 0.9 fusion.35
  0.9 1.6 %fusion.10 = f32[32,1,128]{2,1,0:T(1,128)S(1)} fusion(bf16[32,128,128]{2,1,0:T(8,128)(2,1)} %param.16, bf16[32,128,1]{1,0,2:T(8,128)(2,1)S(1)} %fusion.35), kind=kOutput, calls=%fused_computation.23 | convolution fusion | flops 1048576 | bytes 1073152 | tf_op jit(solution)/shard_map/bp,bps->bs/dot_general | solution.py:249
  2.5 0.7 fusion.30
  3.3 0.8 broadcast_in_dim.9
  4.0 7.3 %all-to-all-start = ((bf16[32,40,128]{2,1,0:T(8,128)(2,1)}), bf16[32,40,128]{2,1,0:T(8,128)(2,1)S(1)}, u32[]{:S(2)}, u32[]{:S(2)}) async-start(bf16[32,40,128]{2,1,0:T(8,128)(2,1)} %broadcast_in_dim.9), calls=%async_computation | async-start | bytes 655360 | tf_op jit(solution)/shard_map/all_to_all | solution.py:258
  11.4 1.5 %constant_dynamic-slice_fusion = bf16[4,2,32,128]{3,2,1,0:T(8,128)(2,1)} fusion(bf16[4,2,256,128]{3,2,1,0:T(8,128)(2,1)} %constant.105.clone, s32[]{:T(128)S(6)} %select_n.46), kind=kLoop, calls=%fused_computation.64 | loop fusion | bytes 131076 | tf_op jit(solution)/shard_map/dynamic_slice | solution.py:281
  12.8 11.5 %copy.30 = f32[2,256,32,128]{3,1,0,2:T(8,128)} copy(f32[2,256,32,128]{3,2,1,0:T(8,128)} %param.22) | data formatting | bytes 16777216 | tf_op args[8]
  24.3 1.1 fusion.5
  25.4 0.8 pad_maximum_fusion.tx_ref
  26.2 0.0 copy-done.9
  26.2 0.0 all-to-all-done
  26.3 0.1 reshape.49.meta_ref
  26.4 8.6 %plan.1 = (f32[64,16,256]{2,1,0:T(8,128)S(1)}, f32[64,8,256]{2,1,0:T(8,128)S(1)}, s32[1,2048]{1,0:T(1,128)S(1)}, s32[2,128]{1,0:T(2,128)S(1)}, s32[1,1024]{1,0:T(1,128)S(1)}) custom-call(f32[8,1024]{1,0:T(8,128)S(1)} %reshape.49.meta_ref, bf16[1024,128]{1,0:T(8,128)(2,1)S(1)} %bitcast.34), custom_call_target="tpu_custom_call" | custom-call | tf_op jit(solution)/shard_map/plan/pallas_call | solution.py:275
  35.1 0.0 copy-start.2
  35.1 1.1 copy-done.2
  36.1 0.8 copy-done.3
  36.9 0.6 copy-done.4
  37.5 0.5 copy-done.5
  38.1 64.9 %field.1.got_ref = f32[64,16,256]{2,1,0:T(8,128)} custom-call(s32[2,128]{1,0:T(2,128)} %copy-done.5, s32[1,2048]{1,0:T(1,128)} %copy-done.4, f32[64,16,256]{2,1,0:T(8,128)} %copy-done.2, f32[64,8,256]{2,1,0:T(8,128)} %copy-done.3, bf16[256,128]{1,0:T(8,128)(2,1)} %bitcast.36, f32[64,8,256]{2,1,0:T(8,128)} %pad_maximum_fusion.tx_ref, ...), custom_call_target="tpu_custom_call" | custom-call | tf_op jit(solution)/shard_map/field/pallas_call | solution.py:309
  103.0 1.2 copy-done.1
  104.2 6.8 %unsort.1 = bf16[1024,128]{1,0:T(8,128)(2,1)} custom-call(f32[64,16,256]{2,1,0:T(8,128)S(1)} %copy-done.1, s32[1,1024]{1,0:T(1,128)S(1)} %get-tuple-element.14.pos_ref), custom_call_target="tpu_custom_call" | custom-call | tf_op jit(solution)/shard_map/unsort/pallas_call | solution.py:317
  111.0 5.8 %all-to-all-start.1 = ((bf16[32,32,128]{2,1,0:T(8,128)(2,1)}), bf16[32,32,128]{2,1,0:T(8,128)(2,1)S(1)}, u32[]{:S(2)}, u32[]{:S(2)}) async-start(bf16[32,32,128]{2,1,0:T(8,128)(2,1)} %bitcast.11), calls=%async_computation.1 | async-start | bytes 524288 | tf_op jit(solution)/shard_map/all_to_all | solution.py:318
  116.8 0.0 copy-done.7
  116.9 0.1 fusion.13
  116.9 0.6 gather_fusion
  117.6 1.2 fusion.6
  118.8 8.7 %all-to-all-done.1 = bf16[32,32,128]{2,1,0:T(8,128)(2,1)S(1)} async-done(((bf16[32,32,128]{2,1,0:T(8,128)(2,1)}), bf16[32,32,128]{2,1,0:T(8,128)(2,1)S(1)}, u32[]{:S(2)}, u32[]{:S(2)}) %all-to-all-start.1) | async-done | bytes 262176 | tf_op jit(solution)/shard_map/all_to_all | solution.py:318
  127.4 0.1 reduce_sum.12
  127.5 0.0 copy-done.6
  127.5 0.6 fusion.8
  128.1 0.9 fusion.1
  (22 shorter events, 0.1 us)
Async XLA Ops:
  0.0 117.6 %copy-start = (bf16[64,128,128]{2,1,0:T(8,128)(2,1)S(1)}, bf16[64,128,128]{2,1,0:T(8,128)(2,1)}, u32[]{:S(2)}) copy-start(bf16[64,128,128]{2,1,0:T(8,128)(2,1)} %param.21) | copy-start | bytes 6291460
  4.0 22.2 %all-to-all-start = ((bf16[32,40,128]{2,1,0:T(8,128)(2,1)}), bf16[32,40,128]{2,1,0:T(8,128)(2,1)S(1)}, u32[]{:S(2)}, u32[]{:S(2)}) async-start(bf16[32,40,128]{2,1,0:T(8,128)(2,1)} %broadcast_in_dim.9), calls=%async_computation | async-start | bytes 655360 | tf_op jit(solution)/shard_map/all_to_all | solution.py:258
  12.8 13.4 %copy-start.9 = (s32[64]{0:T(128)S(1)}, s32[64]{0:T(128)}, u32[]{:S(2)}) copy-start(s32[64]{0:T(128)} %param.20) | copy-start | bytes 772
  35.1 1.1 copy-start.2
  36.1 0.8 copy-start.3
  36.9 0.6 copy-start.4
  37.5 0.5 copy-start.5
  38.1 78.8 %copy-start.7 = (bf16[32,128]{1,0:T(8,128)(2,1)S(1)}, bf16[32,128]{1,0:T(8,128)(2,1)}, u32[]{:S(2)}) copy-start(bf16[32,128]{1,0:T(8,128)(2,1)} %param.14) | copy-start | bytes 24580
  38.1 78.8 %copy-start.8 = (s32[32]{0:T(128)S(1)}, s32[32]{0:T(128)}, u32[]{:S(2)}) copy-start(s32[32]{0:T(128)} %param.15) | copy-start | bytes 388
  103.0 1.2 copy-start.1
  104.2 23.3 %copy-start.6 = (bf16[32,128,128]{2,1,0:T(8,128)(2,1)S(1)}, bf16[32,128,128]{2,1,0:T(8,128)(2,1)}, u32[]{:S(2)}) copy-start(bf16[32,128,128]{2,1,0:T(8,128)(2,1)} %param.16) | copy-start | bytes 3145732
  111.0 17.1 %copy-start.10 = (s32[64]{0:T(128)S(1)}, s32[64]{0:T(128)}, u32[]{:S(2)}) copy-start(s32[64]{0:T(128)} %param.19) | copy-start | bytes 772
  111.0 16.4 %all-to-all-start.1 = ((bf16[32,32,128]{2,1,0:T(8,128)(2,1)}), bf16[32,32,128]{2,1,0:T(8,128)(2,1)S(1)}, u32[]{:S(2)}, u32[]{:S(2)}) async-start(bf16[32,32,128]{2,1,0:T(8,128)(2,1)} %bitcast.11), calls=%async_computation.1 | async-start | bytes 524288 | tf_op jit(solution)/shard_map/all_to_all | solution.py:318

commit v2 on v1

v2 whole, which is shorter than its diff:
```python
import functools
import math

import jax
import jax.numpy as jnp
import ml_dtypes
import numpy as np
from jax import lax
from jax.experimental import pallas as pl
from jax.experimental.pallas import tpu as pltpu
from jax.sharding import PartitionSpec as P

AXES = ("slab", "pen")
CHUNK = 32
BOX_X = 8
LANES = CHUNK * BOX_X
TILE = 8
SLOTS = TILE * CHUNK
f32 = jnp.float32
bf16 = jnp.bfloat16


def halves(table):
    high = table.astype(ml_dtypes.bfloat16)
    low = (table - high.astype(np.float64)).astype(ml_dtypes.bfloat16)
    return high, low


def split(value):
    high = value.astype(bf16)
    return high, (value - high.astype(f32)).astype(bf16)


def dot(a, b):
    return jnp.dot(a, b, preferred_element_type=f32)


def dot_nt(a, b):
    return lax.dot_general(a, b, (((1,), (1,)), ((), ())), preferred_element_type=f32)


def dot_tn(a, b):
    return lax.dot_general(a, b, (((0,), (0,)), ((), ())), preferred_element_type=f32)


def dot3(a_high, a_low, b_high, b_low, mul=dot):
    return mul(a_high, b_high) + (mul(a_high, b_low) + mul(a_low, b_high))


def iota(shape, dim):
    return lax.broadcasted_iota(jnp.int32, shape, dim)


def ones_where(mask):
    return jnp.where(mask, 1.0, 0.0).astype(bf16)


def farm_kernel(
    keep, half, flag_ref, meta_ref, rows_ref, ty_ref, tx_ref, uh_ref, ul_ref, ih_ref, il_ref, kernel_ref,
    out_ref, grid_ref, cols_ref, edge_ref, ex_ref, eh_ref, el_ref, along_ref, kh_ref, sx_ref, yl_ref, got_ref, acc_ref,
    place_ref, boxes_ref, index_ref, cz_ref, xb_ref, kernel_sems, index_sems,
):
    depth, cv, _ = grid_ref.shape
    z_boxes = depth // 4
    nv = cv // 2
    nw = kh_ref.shape[3]
    freqs = kh_ref.shape[2]
    y_boxes = ty_ref.shape[1] // 2
    blocks = rows_ref.shape[0]
    groups = blocks // 128

    copies = []
    for v in range(nv + 1):
        source = 0 if v == nv else 2 * v + flag_ref[0, 0] if half else v
        for part in range(2):
            copies.append(pltpu.make_async_copy(kernel_ref.at[part, :, source, :], kh_ref.at[v, part], kernel_sems.at[v, part]))
    for copy in copies:
        copy.start()

    below = ones_where(iota((128, 128), 0) < iota((128, 128), 1))
    base = jnp.zeros((z_boxes, 128), f32)
    marks, before = [], []
    for g in range(groups):
        box_z = meta_ref[0:1, 128 * g : 128 * g + 128]
        mark = jnp.where(iota((z_boxes, 128), 0) == box_z.astype(jnp.int32), 1.0, 0.0)
        marks.append(mark)
        before.append(base + dot(mark.astype(bf16), below))
        base = base + jnp.sum(mark, axis=1, keepdims=True)
    used = (base.astype(jnp.int32) + (CHUNK - 1)) // CHUNK
    lower = ones_where(iota((z_boxes, z_boxes), 1) < iota((z_boxes, z_boxes), 0))
    start = dot(lower, used.astype(f32).astype(bf16))
    for g in range(groups):
        place = jnp.sum(marks[g] * (start * CHUNK + before[g]), axis=0, keepdims=True)
        place_ref[0:1, 128 * g : 128 * g + 128] = place.astype(jnp.int32)
    end = start.astype(jnp.int32) + used
    for t in range(boxes_ref.shape[1] // 128):
        lane = iota((z_boxes, 128), 1) + 128 * t
        passed = jnp.where(end <= lane, 1, 0)
        boxes_ref[0:1, 128 * t : 128 * t + 128] = jnp.sum(passed, axis=0, keepdims=True)
    boxes_ref[1:2, 0:128] = jnp.sum(used, axis=0, keepdims=True)
    copy = pltpu.make_async_copy(boxes_ref, cz_ref, index_sems.at[0])
    copy.start()
    copy.wait()
    steps = (cz_ref[1, 0] + 1) // 2
    tiles = (2 * steps + TILE - 1) // TILE
    same = iota((128, LANES), 0) % BOX_X == iota((128, LANES), 1) % BOX_X
    wide_of = ones_where(iota((CHUNK, LANES), 0) == iota((CHUNK, LANES), 1) // BOX_X)

    def sort(t, carry):
        hot = ones_where(iota((SLOTS, blocks), 0) + SLOTS * t == place_ref[0:1, :])
        ordered = dot(hot, rows_ref[...]).astype(bf16)
        meta = dot_nt(meta_ref[...].astype(bf16), hot)
        index_ref[0:1, pl.ds(pl.multiple_of(SLOTS * t, SLOTS), SLOTS)] = meta[2:3].astype(jnp.int32)
        meta = meta.astype(bf16)
        for q in range(TILE):
            own = slice(CHUNK * q, CHUNK * q + CHUNK)
            wide = jnp.where(same, dot_tn(ordered[own], wide_of), 0.0)
            sx_ref[TILE * t + q] = jnp.sum(wide.reshape(16, BOX_X, LANES), axis=1)
            yl_ref[TILE * t + q] = dot(meta[:, own], wide_of)
        return carry

    lax.fori_loop(0, tiles, sort, 0)
    copy = pltpu.make_async_copy(index_ref, xb_ref, index_sems.at[1])
    copy.start()
    copy.wait()

    def clear(z, carry):
        grid_ref[z] = jnp.zeros((cv, 2 * nw), f32)
        return carry

    lax.fori_loop(0, depth, clear, 0)
    edge_ref[...] = jnp.zeros_like(edge_ref)

    def tables(c, n):
        for b in range(CHUNK):
            ex_ref[n, BOX_X * b : BOX_X * b + BOX_X, :] = tx_ref[xb_ref[0, CHUNK * c + b]]
        hot = ones_where(iota((y_boxes, LANES), 0) == yl_ref[c][1:2].astype(jnp.int32))
        along = dot(ty_ref[...], jnp.concatenate([hot, hot], axis=0))
        return split(ex_ref[n]), along

    def box_of(c):
        return jnp.minimum(cz_ref[0, c], depth // 4 - 1)

    def scatter(step, carry):
        for n in range(2):
            c = 2 * step + n
            (ex_high, ex_low), along = tables(c, n)
            if keep:
                eh_ref[c], el_ref[c], along_ref[c] = ex_high, ex_low, along
            box = sx_ref[c]
            parts, edges = [], []
            for i in range(4):
                line = [box[4 * i + j : 4 * i + j + 1] for j in range(4)]
                part = along[0:cv] * line[0]
                for j in range(1, 4):
                    part = part + along[cv * j : cv * j + cv] * line[j]
                parts.append(part)
                edges.append((line[0] - line[1]) + (line[2] - line[3]))
            edges.append(jnp.zeros((4, LANES), f32))
            high, low = split(jnp.concatenate(parts + edges, axis=0))
            added = dot3(high, low, ex_high, ex_low)
            where = pl.ds(4 * box_of(c), 4)
            grid_ref[where] = grid_ref[where] + added[: 4 * cv].reshape(4, cv, 2 * nw)
            edge_ref[box_of(c)] = edge_ref[box_of(c)] + added[4 * cv :]
        return carry

    lax.fori_loop(0, steps, scatter, 0)

    def to_columns(g, carry):
        rows = pl.ds(pl.multiple_of(8 * g, 8), 8)
        for z in range(depth // 8):
            piece = grid_ref[8 * z : 8 * z + 8, rows, :]
            cols_ref[rows, 8 * z : 8 * z + 8, :] = jnp.swapaxes(piece, 0, 1)
        return carry

    lax.fori_loop(0, cv // 8, to_columns, 0)

    def filtered(real, imag, kernels):
        field = jnp.concatenate([jnp.concatenate(real, axis=1), jnp.concatenate(imag, axis=1)], axis=0)
        high, low = split(field)
        spec = dot3(uh_ref[...], ul_ref[...], high, low)
        k_re = jnp.concatenate([kh_ref[v, 0] for v in kernels], axis=1)
        k_im = jnp.concatenate([kh_ref[v, 1] for v in kernels], axis=1)
        s_re, s_im = spec[:freqs], spec[freqs:]
        prod = jnp.concatenate([k_re * s_re - k_im * s_im, k_re * s_im + k_im * s_re], axis=0)
        high, low = split(prod)
        back = dot3(ih_ref[...], il_ref[...], high, low)
        return back[:depth], back[depth:]

    def column(p, carry):
        real, imag = [], []
        for v in (2 * p, 2 * p + 1):
            re, im = cols_ref[v], cols_ref[nv + v]
            real.append(re[:, :nw] - im[:, nw:])
            imag.append(re[:, nw:] + im[:, :nw])
        q_re, q_im = filtered(real, imag, (2 * p, 2 * p + 1))
        for n in range(2):
            part = slice(nw * n, nw * n + nw)
            cols_ref[2 * p + n] = jnp.concatenate([q_re[:, part], q_im[:, part]], axis=1)
            cols_ref[nv + 2 * p + n] = jnp.concatenate([q_im[:, part], -q_re[:, part]], axis=1)
        return carry

    for copy in copies:
        copy.wait()
    lax.fori_loop(0, nv // 2, column, 0)

    edge = jnp.concatenate([edge_ref[z][0:4] for z in range(depth // 4)], axis=0)
    q_re, q_im = filtered([edge[:, :nw]], [edge[:, nw:]], (nv,))
    edge = jnp.concatenate([q_re, q_im], axis=1) * flag_ref[0, 1].astype(f32)
    for z in range(depth // 4):
        edge_ref[z, 0:4, :] = edge[4 * z : 4 * z + 4]

    def to_planes(g, carry):
        rows = pl.ds(pl.multiple_of(8 * g, 8), 8)
        for z in range(depth // 8):
            piece = cols_ref[rows, 8 * z : 8 * z + 8, :]
            grid_ref[8 * z : 8 * z + 8, rows, :] = jnp.swapaxes(piece, 0, 1)
        return carry

    lax.fori_loop(0, cv // 8, to_planes, 0)

    def gather(step, carry):
        for n in range(2):
            c = 2 * step + n
            if keep:
                ex_high, ex_low, along = eh_ref[c], el_ref[c], along_ref[c]
            else:
                (ex_high, ex_low), along = tables(c, n)
            planes = grid_ref[pl.ds(4 * box_of(c), 4)].reshape(4 * cv, 2 * nw)
            high, low = split(jnp.concatenate([planes, edge_ref[box_of(c)]], axis=0))
            lines = dot3(high, low, ex_high, ex_low, dot_nt)
            rows = []
            for i in range(4):
                edge = lines[4 * cv + i : 4 * cv + i + 1]
                for j in range(4):
                    row = jnp.sum(along[cv * j : cv * j + cv] * lines[cv * i : cv * i + cv], axis=0, keepdims=True)
                    rows.append(row - edge if j % 2 else row + edge)
            got_ref[c] = jnp.concatenate(rows, axis=0).astype(bf16)
        return carry

    lax.fori_loop(0, steps, gather, 0)

    repeat = ones_where(iota((128, 16), 0) // BOX_X == iota((128, 16), 1))
    acc_ref[...] = jnp.zeros_like(acc_ref)

    def wipe(c, carry):
        got_ref[c] = jnp.zeros((16, LANES), bf16)
        return carry

    lax.fori_loop(2 * steps, TILE * tiles, wipe, 0)

    def unsort(t, carry):
        rows = []
        for q in range(TILE):
            wide = jnp.where(same, dot(repeat, got_ref[TILE * t + q]), 0.0).astype(bf16)
            rows.append(dot_nt(wide_of, wide))
        rows = jnp.concatenate(rows, axis=0).astype(bf16)
        hot = ones_where(iota((SLOTS, blocks), 0) + SLOTS * t == place_ref[0:1, :])
        acc_ref[...] += dot_tn(rows, hot)
        return carry

    lax.fori_loop(0, tiles, unsort, 0)
    for g in range(groups):
        out_ref[128 * g : 128 * g + 128, :] = acc_ref[:, 128 * g : 128 * g + 128].T.astype(bf16)


def turn(length, steps):
    angle = 2.0 * math.pi * (steps % length) / length
    return np.cos(angle), np.sin(angle)


def shards(charges, counts, proj_weight, dest_slab, box_index, pair_target, pair_source, near_matrix, kernel_hat):
    blocks, slots = charges.shape
    stencil = proj_weight.shape[2]
    slab_count = lax.axis_size("slab")
    pen_count = lax.axis_size("pen")
    devices = slab_count * pen_count
    freqs, nv, nw = kernel_hat.shape[1:]
    depth = freqs // 2
    width_y = nv * slab_count
    width_x = nw * pen_count
    planes = freqs // slab_count
    rows_pen = width_y // pen_count
    total_blocks = blocks * devices
    z_boxes, y_boxes, x_boxes = depth // 4, width_y // 4, width_x // BOX_X
    chunks = -(-(total_blocks // CHUNK + z_boxes) // TILE) * TILE
    factor = 1.0 / math.sqrt(float(freqs) * width_y * width_x * total_blocks * stencil)
    slab, pen = lax.axis_index("slab"), lax.axis_index("pen")

    live = jnp.arange(slots, dtype=jnp.int32)[None, :] < counts[:, None]
    charge = jnp.where(live, charges, jnp.zeros_like(charges))
    spread = jnp.einsum("bp,bps->bs", charge, proj_weight, preferred_element_type=f32)

    per_plane = rows_pen // 4 * x_boxes
    box_z = dest_slab[:, 0] * (planes // 4) + box_index // per_plane
    box_y = pen * (rows_pen // 4) + box_index // x_boxes % (rows_pen // 4)
    box_x = box_index % x_boxes
    meta = jnp.stack([box_z, box_y, box_x]).astype(bf16)
    meta = jnp.pad(meta, ((0, 5), (0, stencil - blocks)))
    packet = jnp.concatenate([spread.astype(bf16), meta], axis=0)
    packets = lax.all_to_all(jnp.broadcast_to(packet, (devices,) + packet.shape), AXES, 0, 0, tiled=True)
    rows = packets[:, :blocks].reshape(total_blocks, stencil)
    boxes = packets[:, blocks:, :blocks].transpose(1, 0, 2).reshape(8, total_blocks).astype(f32)

    v_all, yb_all = np.arange(width_y), np.arange(y_boxes)
    cos, sin = turn(width_y, v_all[None, :, None] * (4 * yb_all[None, None, :] + np.arange(4)[:, None, None]))
    half = nv % 8 == 0
    scale = np.where((v_all == 0) | (not half), 1.0, math.sqrt(2.0))[None, :, None]
    high, low = halves(np.stack([cos * scale, -sin * scale], axis=1))
    along = np.concatenate([high, low], axis=3)
    odd = slab >= slab_count // 2
    own = nv // 2 if half else nv
    if half:
        along = jnp.where(odd, jnp.asarray(along[:, :, 1::2]), jnp.asarray(along[:, :, 0::2]))
    ty = lax.dynamic_slice_in_dim(jnp.asarray(along), slab * own, own, 2).reshape(8 * own, 2 * y_boxes)

    x_all = jnp.arange(width_x, dtype=jnp.int32)[:, None]
    w_own = pen * nw + jnp.arange(nw, dtype=jnp.int32)[None, :]
    phase = (x_all * w_own % width_x).astype(f32) * (2.0 * math.pi / width_x)
    tx = jnp.concatenate([jnp.cos(phase), -jnp.sin(phase)], axis=1).reshape(x_boxes, BOX_X, 2 * nw)

    cos, sin = turn(freqs, np.arange(freqs)[:, None] * np.arange(depth)[None, :])
    forth = np.block([[cos, sin], [-sin, cos]])
    uh, ul = halves(forth)
    ih, il = halves(forth.T * factor)
    last = jnp.logical_and(half, slab == slab_count // 2)
    flags = jnp.stack([odd, last]).astype(jnp.int32)[None, :]
    keep = chunks <= 64
    kept = chunks if keep else 1
    vmem = pl.BlockSpec(memory_space=pltpu.VMEM)
    smem = pl.BlockSpec(memory_space=pltpu.SMEM)
    lane_tiles = -(-chunks // 128) * 128
    farm = pl.pallas_call(
        functools.partial(farm_kernel, keep, half),
        out_shape=jax.ShapeDtypeStruct((total_blocks, stencil), bf16),
        in_specs=[smem] + [vmem] * 8 + [pl.BlockSpec(memory_space=pl.ANY)],
        out_specs=vmem,
        scratch_shapes=[
            pltpu.VMEM((depth, 2 * own, 2 * nw), f32),
            pltpu.VMEM((2 * own, depth, 2 * nw), f32),
            pltpu.VMEM((z_boxes, 8, 2 * nw), f32),
            pltpu.VMEM((2, LANES, 2 * nw), f32),
            pltpu.VMEM((kept, LANES, 2 * nw), bf16),
            pltpu.VMEM((kept, LANES, 2 * nw), bf16),
            pltpu.VMEM((kept, 8 * own, LANES), f32),
            pltpu.VMEM((own + 1, 2, freqs, nw), f32),
            pltpu.VMEM((chunks, 16, LANES), f32),
            pltpu.VMEM((chunks, 8, LANES), f32),
            pltpu.VMEM((chunks, 16, LANES), bf16),
            pltpu.VMEM((stencil, total_blocks), f32),
            pltpu.VMEM((1, total_blocks), jnp.int32),
            pltpu.VMEM((2, lane_tiles), jnp.int32),
            pltpu.VMEM((1, chunks * CHUNK), jnp.int32),
            pltpu.SMEM((2, lane_tiles), jnp.int32),
            pltpu.SMEM((1, chunks * CHUNK), jnp.int32),
            pltpu.SemaphoreType.DMA((own + 1, 2)),
            pltpu.SemaphoreType.DMA((2,)),
        ],
        compiler_params=pltpu.CompilerParams(vmem_limit_bytes=58 << 20),
        name="farm",
    )
    partial = farm(flags, boxes, rows, ty, tx, jnp.asarray(uh), jnp.asarray(ul), jnp.asarray(ih), jnp.asarray(il), kernel_hat)
    shares = lax.all_to_all(partial.reshape(devices, blocks, stencil), AXES, 0, 0, tiled=True)
    samples = jnp.sum(shares.astype(f32), axis=0).astype(bf16)

    far = jnp.einsum("bps,bs->bp", proj_weight, samples, preferred_element_type=f32)
    driven = charge[pair_source]
    terms = jnp.einsum("tpq,tq->tp", near_matrix, driven, preferred_element_type=f32)
    owners = (pair_target[:, None] == jnp.arange(blocks, dtype=jnp.int32)[None, :]).astype(f32)
    near = jnp.einsum("tb,tp->bp", owners, terms, precision=lax.Precision.HIGHEST)
    total = jnp.where(live, far + near, jnp.zeros_like(far))
    return total.astype(bf16)


def solution(mesh):
    placed = (
        P(AXES, None),
        P(AXES),
        P(AXES, None, None),
        P(AXES, None),
        P(AXES),
        P(AXES),
        P(AXES),
        P(AXES, None, None),
        P(None, None, "slab", "pen"),
    )
    return jax.shard_map(shards, mesh=mesh, in_specs=placed, out_specs=P(AXES, None), check_vma=False)
```

time: 129 us -> 91.7 us (0.71)
  Pallas kernels: 80.3 us -> 51.1 us
  local copies, waits for them, and re-layouts: 18.7 us -> 2.89 us
  waiting for transfers between devices: 8.68 us -> 16.7 us
  starting transfers between devices: 13.1 us -> 10 us
  other arithmetic: 3.74 us -> 5.74 us
    pallas_call x3 -> x1, Pallas kernels: 80.3 us -> 51.1 us  [shards(): farm(flags, boxes, rows, ty, tx, jnp.asarray(uh), jnp.asarray(ul), jnp.as...]
    unnamed x23 -> x12, local copies, waits for them, and re-layouts: 15.7 us -> 0.03 us
    all_to_all x1, waiting for transfers between devices: 0.01 us -> 8.02 us  [shards(): lax.all_to_all(jnp.broadcast_to(packet, (devices,) + packet.shape), AXES,...]
    all_to_all x1, starting transfers between devices: 5.83 us -> 2.73 us  [shards(): lax.all_to_all(partial.reshape(devices, blocks, stencil), AXES, 0, 0, til...]
    dynamic_slice x1 -> x0, local copies, waits for them, and re-layouts: 1.46 us -> none  [shards(): lax.dynamic_slice_in_dim(jnp.asarray(along), slab * nv, nv, 2)]
    select_n x0 -> x1, other arithmetic: none -> 1.41 us  [shards(): jnp.where(odd, jnp.asarray(along[:, :, 1::2]), jnp.asarray(along[:, :, 0:...]
  transfers between devices with their start and end apart: 2 -> 2, of which waited for: 1 -> 2; matrix products, arithmetic and copies ran while one was open for 13% -> 6% of each run, Pallas kernels for 0% -> 0%
where the time goes in v2:
time: 91.7 us; the launch traced here: 90.9 us
  Pallas kernels  51.1 us (56%)
  waiting for transfers between devices  16.7 us (18%)
  starting transfers between devices  10 us (11%)
  other arithmetic  5.74 us (6%)
  matrix products  4.3 us (5%)
  local copies, waits for them, and re-layouts  2.89 us (3%)
    pallas_call x1, Pallas kernels, shards(): farm(flags, boxes, rows, ty, tx, jnp.asarray(uh), jnp.asarray(ul), jnp.as...  51.1 us
    all_to_all x1, waiting for transfers between devices, shards(): lax.all_to_all(partial.reshape(devices, blocks, stencil), AXES, 0, 0, til...  8.67 us
    all_to_all x1, waiting for transfers between devices, shards(): lax.all_to_all(jnp.broadcast_to(packet, (devices,) + packet.shape), AXES,...  8.02 us
    all_to_all x1, starting transfers between devices, shards(): lax.all_to_all(jnp.broadcast_to(packet, (devices,) + packet.shape), AXES,...  7.3 us
    all_to_all x1, starting transfers between devices, shards(): lax.all_to_all(partial.reshape(devices, blocks, stencil), AXES, 0, 0, til...  2.73 us
  transfers between devices with their start and end apart: 2, of which 2 were waited for; matrix products, arithmetic and copies ran while one was open for 6% of the time, Pallas kernels for 0%

profile of v2, /device:TPU:0, one launch (start us, length us, event | category | flops | bytes accessed | tf_op | source)
XLA Modules:
  0.0 90.9 jit_solution(10212983307354702945)
XLA Ops:
  0.0 0.0 copy-start
  0.0 0.0 copy-start.4
  0.0 0.9 %fusion.35 = bf16[32,128,1]{1,0,2:T(8,128)(2,1)S(1)} fusion(bf16[32,128]{1,0:T(8,128)(2,1)} %param.15, s32[32]{0:T(128)} %param.16), kind=kLoop, calls=%fused_computation.65 | loop fusion | flops 8192 | bytes 16512 | tf_op jit(solution)/shard_map/jit(_where)/select_n | solution.py:291
  0.9 1.6 %fusion.10 = f32[32,1,128]{2,1,0:T(1,128)S(1)} fusion(bf16[32,128,128]{2,1,0:T(8,128)(2,1)} %param.17, bf16[32,128,1]{1,0,2:T(8,128)(2,1)S(1)} %fusion.35), kind=kOutput, calls=%fused_computation.23 | convolution fusion | flops 1048576 | bytes 1073152 | tf_op jit(solution)/shard_map/bp,bps->bs/dot_general | solution.py:292
  2.5 0.7 fusion.30
  3.3 0.8 broadcast_in_dim.9
  4.1 7.3 %all-to-all-start = ((bf16[32,40,128]{2,1,0:T(8,128)(2,1)}), bf16[32,40,128]{2,1,0:T(8,128)(2,1)S(1)}, u32[]{:S(2)}, u32[]{:S(2)}) async-start(bf16[32,40,128]{2,1,0:T(8,128)(2,1)} %broadcast_in_dim.9), calls=%async_computation | async-start | bytes 655360 | tf_op jit(solution)/shard_map/all_to_all | solution.py:301
  11.4 1.4 %dynamic-slice_select_fusion = bf16[4,2,16,128]{3,2,1,0:T(8,128)(2,1)} fusion(bf16[4,2,128,128]{3,2,1,0:T(8,128)(2,1)} %constant.107.clone, s32[]{:T(128)S(6)} %select_n.56, bf16[4,2,128,128]{3,2,1,0:T(8,128)(2,1)} %constant.106.clone, pred[]{:T(512)} %ge.3), kind=kLoop, calls=%fused_computation.16 | loop fusion | flops 16384 | bytes 98309 | tf_op jit(solution)/shard_map/jit(_where)/select_n | solution.py:314
  12.8 0.6 add_convert_fusion.flag_ref
  13.4 1.1 %fusion.5 = (f32[64,8,128]{2,1,0:T(8,128)S(1)}, f32[64,8,128]{2,1,0:T(8,128)S(1)}) fusion(s32[128]{0:T(128)S(1)} %iota_add_fusion, s32[64,8]{1,0:T(8,128)S(1)} %multiply_add_fusion), kind=kLoop, calls=%fused_computation.15 | loop fusion | flops 983040 | bytes 526848 | tf_op jit(solution)/shard_map/cos | solution.py:320
  14.5 0.8 pad_maximum_fusion.tx_ref
  15.3 0.0 copy-done.4
  15.3 8.0 %all-to-all-done = bf16[32,40,128]{2,1,0:T(8,128)(2,1)S(1)} async-done(((bf16[32,40,128]{2,1,0:T(8,128)(2,1)}), bf16[32,40,128]{2,1,0:T(8,128)(2,1)S(1)}, u32[]{:S(2)}, u32[]{:S(2)}) %all-to-all-start) | async-done | bytes 327712 | tf_op jit(solution)/shard_map/all_to_all | solution.py:301
  23.4 0.7 reshape.80.meta_ref
  24.1 0.7 slice.11
  24.8 0.0 copy-start.2
  24.8 51.1 %farm.1 = bf16[1024,128]{1,0:T(8,128)(2,1)} custom-call(s32[1,2]{1,0:T(1,128)} %add_convert_fusion.flag_ref, f32[8,1024]{1,0:T(8,128)} %reshape.80.meta_ref, bf16[1024,128]{1,0:T(8,128)(2,1)} %bitcast.34, bf16[128,128]{1,0:T(8,128)(2,1)} %bitcast.36, f32[64,8,256]{2,1,0:T(8,128)} %pad_maximum_fusion.tx_ref, bf16[512,256]{1,0:T(8,128)(2,1)} %constant.108.clone.uh_ref, ...), custom_call_target="tpu_custom_call" | custom-call | tf_op jit(solution)/shard_map/farm/pallas_call | solution.py:362
  75.9 0.0 copy-start.1
  75.9 0.0 copy-start.5
  75.9 2.7 %all-to-all-start.1 = ((bf16[32,32,128]{2,1,0:T(8,128)(2,1)}), bf16[32,32,128]{2,1,0:T(8,128)(2,1)S(1)}, u32[]{:S(2)}, u32[]{:S(2)}) async-start(bf16[32,32,128]{2,1,0:T(8,128)(2,1)} %bitcast.33), calls=%async_computation.1 | async-start | bytes 524288 | tf_op jit(solution)/shard_map/all_to_all | solution.py:363
  78.7 0.0 copy-done.2
  78.7 0.0 copy-done.3
  78.7 0.1 fusion.13
  78.8 0.6 gather_fusion
  79.4 0.0 copy-done
  79.4 1.2 %fusion.6 = f32[64,1,128]{2,1,0:T(1,128)S(1)} fusion(bf16[64,128,128]{2,1,0:T(8,128)(2,1)S(1)} %copy-done, bf16[64,128,1]{1,0,2:T(8,128)(2,1)S(1)} %bitcast.35), kind=kOutput, calls=%fused_computation.17 | convolution fusion | flops 2097152 | bytes 2146304 | tf_op jit(solution)/shard_map/tpq,tq->tp/dot_general | solution.py:368
  80.6 8.7 %all-to-all-done.1 = bf16[32,32,128]{2,1,0:T(8,128)(2,1)S(1)} async-done(((bf16[32,32,128]{2,1,0:T(8,128)(2,1)}), bf16[32,32,128]{2,1,0:T(8,128)(2,1)S(1)}, u32[]{:S(2)}, u32[]{:S(2)}) %all-to-all-start.1) | async-done | bytes 262176 | tf_op jit(solution)/shard_map/all_to_all | solution.py:363
  89.3 0.1 reduce_sum.12
  89.3 0.0 copy-done.1
  89.3 0.6 fusion.8
  90.0 0.0 copy-done.5
  90.0 0.9 fusion.1
  (10 shorter events, 0.1 us)
Async XLA Ops:
  0.0 79.4 %copy-start = (bf16[64,128,128]{2,1,0:T(8,128)(2,1)S(1)}, bf16[64,128,128]{2,1,0:T(8,128)(2,1)}, u32[]{:S(2)}) copy-start(bf16[64,128,128]{2,1,0:T(8,128)(2,1)} %param.22) | copy-start | bytes 6291460
  0.0 15.3 %copy-start.4 = (s32[64]{0:T(128)S(1)}, s32[64]{0:T(128)}, u32[]{:S(2)}) copy-start(s32[64]{0:T(128)} %param.21) | copy-start | bytes 772
  4.1 19.3 %all-to-all-start = ((bf16[32,40,128]{2,1,0:T(8,128)(2,1)}), bf16[32,40,128]{2,1,0:T(8,128)(2,1)S(1)}, u32[]{:S(2)}, u32[]{:S(2)}) async-start(bf16[32,40,128]{2,1,0:T(8,128)(2,1)} %broadcast_in_dim.9), calls=%async_computation | async-start | bytes 655360 | tf_op jit(solution)/shard_map/all_to_all | solution.py:301
  24.8 53.9 %copy-start.2 = (bf16[32,128]{1,0:T(8,128)(2,1)S(1)}, bf16[32,128]{1,0:T(8,128)(2,1)}, u32[]{:S(2)}) copy-start(bf16[32,128]{1,0:T(8,128)(2,1)} %param.15) | copy-start | bytes 24580
  24.8 53.9 %copy-start.3 = (s32[32]{0:T(128)S(1)}, s32[32]{0:T(128)}, u32[]{:S(2)}) copy-start(s32[32]{0:T(128)} %param.16) | copy-start | bytes 388
  75.9 13.4 %copy-start.1 = (bf16[32,128,128]{2,1,0:T(8,128)(2,1)S(1)}, bf16[32,128,128]{2,1,0:T(8,128)(2,1)}, u32[]{:S(2)}) copy-start(bf16[32,128,128]{2,1,0:T(8,128)(2,1)} %param.17) | copy-start | bytes 3145732
  75.9 14.0 %copy-start.5 = (s32[64]{0:T(128)S(1)}, s32[64]{0:T(128)}, u32[]{:S(2)}) copy-start(s32[64]{0:T(128)} %param.20) | copy-start | bytes 772
  75.9 13.3 %all-to-all-start.1 = ((bf16[32,32,128]{2,1,0:T(8,128)(2,1)}), bf16[32,32,128]{2,1,0:T(8,128)(2,1)S(1)}, u32[]{:S(2)}, u32[]{:S(2)}) async-start(bf16[32,32,128]{2,1,0:T(8,128)(2,1)} %bitcast.33), calls=%async_computation.1 | async-start | bytes 524288 | tf_op jit(solution)/shard_map/all_to_all | solution.py:363

commit v3 on v2

--- a/solution.py
+++ b/solution.py
@@ -43,8 +43,32 @@
     return lax.dot_general(a, b, (((0,), (0,)), ((), ())), preferred_element_type=f32)
 
 
-def dot3(a_high, a_low, b_high, b_low, mul=dot):
-    return mul(a_high, b_high) + (mul(a_high, b_low) + mul(a_low, b_high))
+def dot3(a_high, a_low, b_high, b_low):
+    left = jnp.concatenate([a_high, a_high, a_low], axis=1)
+    return dot(left, jnp.concatenate([b_high, b_low, b_high], axis=0))
+
+
+def stacked(mul, a_high, a_low, b_high, b_low):
+    rows = a_high.shape[0]
+    both = mul(jnp.concatenate([a_high, a_low], axis=0), b_high)
+    return both[:rows] + (both[rows:] + mul(a_high, b_low))
+
+
+def row_sums(parts):
+    order = [parts[n] for n in (0, 4, 2, 6, 1, 5, 3, 7)]
+    for step in (4, 2, 1):
+        first = iota(order[0].shape, 0) % (2 * step) < step
+        merged = []
+        for a, b in zip(order[0::2], order[1::2]):
+            kept = jnp.where(first, a, b)
+            moved = jnp.where(first, b, a)
+            merged.append(kept + (pltpu.roll(moved, 4, 0) if step == 4 else swap_rows(moved, step, first)))
+        order = merged
+    return order[0]
+
+
+def swap_rows(value, step, first):
+    return jnp.where(first, pltpu.roll(value, 8 - step, 0), pltpu.roll(value, step, 0))
 
 
 def iota(shape, dim):
@@ -103,20 +127,27 @@
     copy.wait()
     steps = (cz_ref[1, 0] + 1) // 2
     tiles = (2 * steps + TILE - 1) // TILE
-    same = iota((128, LANES), 0) % BOX_X == iota((128, LANES), 1) % BOX_X
-    wide_of = ones_where(iota((CHUNK, LANES), 0) == iota((CHUNK, LANES), 1) // BOX_X)
+    row, col = iota((LANES, LANES), 0), iota((LANES, LANES), 1)
+    to_lanes = ones_where((row // CHUNK == col % BOX_X) & (row % CHUNK == col // BOX_X))
+    from_lanes = ones_where((col // CHUNK == row % BOX_X) & (col % CHUNK == row // BOX_X))
+    row, col = iota((128, 128), 0), iota((128, 128), 1)
+    points_first = ones_where((row // 16 == col % BOX_X) & (row % 16 == col // BOX_X))
 
     def sort(t, carry):
         hot = ones_where(iota((SLOTS, blocks), 0) + SLOTS * t == place_ref[0:1, :])
         ordered = dot(hot, rows_ref[...]).astype(bf16)
+        turned = dot_nt(points_first, ordered)
+        lines = exchanged([turned[16 * k : 16 * k + 16] for k in range(BOX_X)])
+        lines = dot(jnp.concatenate(lines, axis=0).astype(bf16), to_lanes)
+        sx_ref[pl.ds(TILE * t, TILE)] = lines.reshape(TILE, 16, LANES)
         meta = dot_nt(meta_ref[...].astype(bf16), hot)
         index_ref[0:1, pl.ds(pl.multiple_of(SLOTS * t, SLOTS), SLOTS)] = meta[2:3].astype(jnp.int32)
-        meta = meta.astype(bf16)
-        for q in range(TILE):
-            own = slice(CHUNK * q, CHUNK * q + CHUNK)
-            wide = jnp.where(same, dot_tn(ordered[own], wide_of), 0.0)
-            sx_ref[TILE * t + q] = jnp.sum(wide.reshape(16, BOX_X, LANES), axis=1)
-            yl_ref[TILE * t + q] = dot(meta[:, own], wide_of)
+        owned = jnp.where(iota((TILE, SLOTS), 1) // CHUNK == iota((TILE, SLOTS), 0), meta[1:2], 0.0)
+        owned = owned[:, :128] + owned[:, 128:]
+        owned = owned + pltpu.roll(owned, 64, 1)
+        owned = owned + pltpu.roll(owned, 32, 1)
+        owned = jnp.concatenate([owned, owned], axis=1).astype(bf16)
+        yl_ref[pl.ds(pl.multiple_of(TILE * t, TILE), TILE), :] = dot(owned, to_lanes)
         return carry
 
     lax.fori_loop(0, tiles, sort, 0)
@@ -134,7 +165,7 @@
     def tables(c, n):
         for b in range(CHUNK):
             ex_ref[n, BOX_X * b : BOX_X * b + BOX_X, :] = tx_ref[xb_ref[0, CHUNK * c + b]]
-        hot = ones_where(iota((y_boxes, LANES), 0) == yl_ref[c][1:2].astype(jnp.int32))
+        hot = ones_where(iota((y_boxes, LANES), 0) == yl_ref[pl.ds(c, 1), :].astype(jnp.int32))
         along = dot(ty_ref[...], jnp.concatenate([hot, hot], axis=0))
         return split(ex_ref[n]), along
 
@@ -158,7 +189,7 @@
                 edges.append((line[0] - line[1]) + (line[2] - line[3]))
             edges.append(jnp.zeros((4, LANES), f32))
             high, low = split(jnp.concatenate(parts + edges, axis=0))
-            added = dot3(high, low, ex_high, ex_low)
+            added = stacked(dot, high, low, ex_high, ex_low)
             where = pl.ds(4 * box_of(c), 4)
             grid_ref[where] = grid_ref[where] + added[: 4 * cv].reshape(4, cv, 2 * nw)
             edge_ref[box_of(c)] = edge_ref[box_of(c)] + added[4 * cv :]
@@ -187,22 +218,23 @@
         back = dot3(ih_ref[...], il_ref[...], high, low)
         return back[:depth], back[depth:]
 
-    def column(p, carry):
-        real, imag = [], []
-        for v in (2 * p, 2 * p + 1):
-            re, im = cols_ref[v], cols_ref[nv + v]
-            real.append(re[:, :nw] - im[:, nw:])
-            imag.append(re[:, nw:] + im[:, :nw])
-        q_re, q_im = filtered(real, imag, (2 * p, 2 * p + 1))
-        for n in range(2):
-            part = slice(nw * n, nw * n + nw)
-            cols_ref[2 * p + n] = jnp.concatenate([q_re[:, part], q_im[:, part]], axis=1)
-            cols_ref[nv + 2 * p + n] = jnp.concatenate([q_im[:, part], -q_re[:, part]], axis=1)
+    def column(step, carry):
+        for p in (2 * step, 2 * step + 1):
+            real, imag = [], []
+            for v in (2 * p, 2 * p + 1):
+                re, im = cols_ref[v], cols_ref[nv + v]
+                real.append(re[:, :nw] - im[:, nw:])
+                imag.append(re[:, nw:] + im[:, :nw])
+            q_re, q_im = filtered(real, imag, (2 * p, 2 * p + 1))
+            for n in range(2):
+                part = slice(nw * n, nw * n + nw)
+                cols_ref[2 * p + n] = jnp.concatenate([q_re[:, part], q_im[:, part]], axis=1)
+                cols_ref[nv + 2 * p + n] = jnp.concatenate([q_im[:, part], -q_re[:, part]], axis=1)
         return carry
 
     for copy in copies:
         copy.wait()
-    lax.fori_loop(0, nv // 2, column, 0)
+    lax.fori_loop(0, nv // 4, column, 0)
 
     edge = jnp.concatenate([edge_ref[z][0:4] for z in range(depth // 4)], axis=0)
     q_re, q_im = filtered([edge[:, :nw]], [edge[:, nw:]], (nv,))
@@ -228,19 +260,24 @@
                 (ex_high, ex_low), along = tables(c, n)
             planes = grid_ref[pl.ds(4 * box_of(c), 4)].reshape(4 * cv, 2 * nw)
             high, low = split(jnp.concatenate([planes, edge_ref[box_of(c)]], axis=0))
-            lines = dot3(high, low, ex_high, ex_low, dot_nt)
-            rows = []
-            for i in range(4):
-                edge = lines[4 * cv + i : 4 * cv + i + 1]
-                for j in range(4):
-                    row = jnp.sum(along[cv * j : cv * j + cv] * lines[cv * i : cv * i + cv], axis=0, keepdims=True)
-                    rows.append(row - edge if j % 2 else row + edge)
-            got_ref[c] = jnp.concatenate(rows, axis=0).astype(bf16)
+            lines = stacked(dot_nt, high, low, ex_high, ex_low)
+            got = []
+            for i in (0, 2):
+                parts = []
+                for n in range(8):
+                    at, j = i + n // 4, n % 4
+                    part = along[cv * j : cv * j + cv] * lines[cv * at : cv * at + cv]
+                    parts.append(jnp.sum(part.reshape(cv // 8, 8, LANES), axis=0))
+                first = lines[4 * cv + i : 4 * cv + i + 1]
+                second = lines[4 * cv + i + 1 : 4 * cv + i + 2]
+                edge = jnp.where(iota((8, LANES), 0) < 4, first, second)
+                edge = jnp.where(iota((8, LANES), 0) % 2 == 0, edge, -edge)
+                got.append(row_sums(parts) + edge)
+            got_ref[c] = jnp.concatenate(got, axis=0).astype(bf16)
         return carry
 
     lax.fori_loop(0, steps, gather, 0)
 
-    repeat = ones_where(iota((128, 16), 0) // BOX_X == iota((128, 16), 1))
     acc_ref[...] = jnp.zeros_like(acc_ref)
 
     def wipe(c, carry):
@@ -250,18 +287,34 @@
     lax.fori_loop(2 * steps, TILE * tiles, wipe, 0)
 
     def unsort(t, carry):
-        rows = []
-        for q in range(TILE):
-            wide = jnp.where(same, dot(repeat, got_ref[TILE * t + q]), 0.0).astype(bf16)
-            rows.append(dot_nt(wide_of, wide))
-        rows = jnp.concatenate(rows, axis=0).astype(bf16)
+        lines = got_ref[pl.ds(TILE * t, TILE)].reshape(TILE * 16, LANES)
+        lines = dot(lines, from_lanes)
+        rows = exchanged([lines[16 * q : 16 * q + 16] for q in range(TILE)])
         hot = ones_where(iota((SLOTS, blocks), 0) + SLOTS * t == place_ref[0:1, :])
-        acc_ref[...] += dot_tn(rows, hot)
+        acc_ref[...] += dot(jnp.concatenate(rows, axis=0).astype(bf16), hot)
         return carry
 
     lax.fori_loop(0, tiles, unsort, 0)
     for g in range(groups):
-        out_ref[128 * g : 128 * g + 128, :] = acc_ref[:, 128 * g : 128 * g + 128].T.astype(bf16)
+        part = acc_ref[:, 128 * g : 128 * g + 128].astype(bf16)
+        out_ref[128 * g : 128 * g + 128, :] = dot_tn(part, points_first).astype(bf16)
+
+
+def exchanged(lines):
+    lane = iota((16, 128), 1) // CHUNK
+    results = []
+    for q in range(8):
+        tiles = []
+        for h in range(2):
+            tile = None
+            for a in range(4):
+                piece = lines[4 * h + a][:, 128 * (q // 4) : 128 * (q // 4) + 128]
+                shift = CHUNK * (a - q % 4) % 128
+                piece = pltpu.roll(piece, shift, 1) if shift else piece
+                tile = piece if tile is None else jnp.where(lane == a, piece, tile)
+            tiles.append(tile)
+        results.append(jnp.concatenate(tiles, axis=1))
+    return results
 
 
 def turn(length, steps):
@@ -345,7 +398,7 @@
             pltpu.VMEM((kept, 8 * own, LANES), f32),
             pltpu.VMEM((own + 1, 2, freqs, nw), f32),
             pltpu.VMEM((chunks, 16, LANES), f32),
-            pltpu.VMEM((chunks, 8, LANES), f32),
+            pltpu.VMEM((chunks, LANES), f32),
             pltpu.VMEM((chunks, 16, LANES), bf16),
             pltpu.VMEM((stencil, total_blocks), f32),
             pltpu.VMEM((1, total_blocks), jnp.int32),

time: 91.7 us -> 83.4 us (0.909)
  Pallas kernels: 51.1 us -> 42.8 us
    pallas_call x1, Pallas kernels: 51.1 us -> 42.8 us  [shards(): farm(flags, boxes, rows, ty, tx, jnp.asarray(uh), jnp.asarray(ul), jnp.as...]
  transfers between devices with their start and end apart: 2 -> 2, of which waited for: 2 -> 2; matrix products, arithmetic and copies ran while one was open for 6% -> 7% of each run, Pallas kernels for 0% -> 0%
where the time goes in v3:
time: 83.4 us; the launch traced here: 82.6 us
  Pallas kernels  42.8 us (51%)
  waiting for transfers between devices  16.7 us (20%)
  starting transfers between devices  10 us (12%)
  other arithmetic  5.74 us (7%)
  matrix products  4.3 us (5%)
  local copies, waits for them, and re-layouts  2.89 us (3%)
    pallas_call x1, Pallas kernels, shards(): farm(flags, boxes, rows, ty, tx, jnp.asarray(uh), jnp.asarray(ul), jnp.as...  42.8 us
    all_to_all x1, waiting for transfers between devices, shards(): lax.all_to_all(partial.reshape(devices, blocks, stencil), AXES, 0, 0, til...  8.67 us
    all_to_all x1, waiting for transfers between devices, shards(): lax.all_to_all(jnp.broadcast_to(packet, (devices,) + packet.shape), AXES,...  8.02 us
    all_to_all x1, starting transfers between devices, shards(): lax.all_to_all(jnp.broadcast_to(packet, (devices,) + packet.shape), AXES,...  7.3 us
    all_to_all x1, starting transfers between devices, shards(): lax.all_to_all(partial.reshape(devices, blocks, stencil), AXES, 0, 0, til...  2.73 us
  transfers between devices with their start and end apart: 2, of which 2 were waited for; matrix products, arithmetic and copies ran while one was open for 7% of the time, Pallas kernels for 0%

profile of v3, /device:TPU:0, one launch (start us, length us, event | category | flops | bytes accessed | tf_op | source)
XLA Modules:
  0.0 82.6 jit_solution(8066518932184646609)
XLA Ops:
  0.0 0.0 copy-start
  0.0 0.0 copy-start.4
  0.0 0.9 %fusion.35 = bf16[32,128,1]{1,0,2:T(8,128)(2,1)S(1)} fusion(bf16[32,128]{1,0:T(8,128)(2,1)} %param.15, s32[32]{0:T(128)} %param.16), kind=kLoop, calls=%fused_computation.65 | loop fusion | flops 8192 | bytes 16512 | tf_op jit(solution)/shard_map/jit(_where)/select_n | solution.py:344
  0.9 1.6 %fusion.10 = f32[32,1,128]{2,1,0:T(1,128)S(1)} fusion(bf16[32,128,128]{2,1,0:T(8,128)(2,1)} %param.17, bf16[32,128,1]{1,0,2:T(8,128)(2,1)S(1)} %fusion.35), kind=kOutput, calls=%fused_computation.23 | convolution fusion | flops 1048576 | bytes 1073152 | tf_op jit(solution)/shard_map/bp,bps->bs/dot_general | solution.py:345
  2.5 0.7 fusion.30
  3.3 0.8 broadcast_in_dim.9
  4.1 7.3 %all-to-all-start = ((bf16[32,40,128]{2,1,0:T(8,128)(2,1)}), bf16[32,40,128]{2,1,0:T(8,128)(2,1)S(1)}, u32[]{:S(2)}, u32[]{:S(2)}) async-start(bf16[32,40,128]{2,1,0:T(8,128)(2,1)} %broadcast_in_dim.9), calls=%async_computation | async-start | bytes 655360 | tf_op jit(solution)/shard_map/all_to_all | solution.py:354
  11.4 1.4 %dynamic-slice_select_fusion = bf16[4,2,16,128]{3,2,1,0:T(8,128)(2,1)} fusion(bf16[4,2,128,128]{3,2,1,0:T(8,128)(2,1)} %constant.107.clone, s32[]{:T(128)S(6)} %select_n.56, bf16[4,2,128,128]{3,2,1,0:T(8,128)(2,1)} %constant.106.clone, pred[]{:T(512)} %ge.3), kind=kLoop, calls=%fused_computation.16 | loop fusion | flops 16384 | bytes 98309 | tf_op jit(solution)/shard_map/jit(_where)/select_n | solution.py:367
  12.8 0.6 add_convert_fusion.flag_ref
  13.4 1.1 %fusion.5 = (f32[64,8,128]{2,1,0:T(8,128)S(1)}, f32[64,8,128]{2,1,0:T(8,128)S(1)}) fusion(s32[128]{0:T(128)S(1)} %iota_add_fusion, s32[64,8]{1,0:T(8,128)S(1)} %multiply_add_fusion), kind=kLoop, calls=%fused_computation.15 | loop fusion | flops 983040 | bytes 526848 | tf_op jit(solution)/shard_map/cos | solution.py:373
  14.5 0.8 %pad_maximum_fusion.tx_ref = f32[64,8,256]{2,1,0:T(8,128)} fusion(f32[64,8,128]{2,1,0:T(8,128)S(1)} %get-tuple-element.6, f32[64,8,128]{2,1,0:T(8,128)S(1)} %get-tuple-element.5), kind=kLoop, calls=%fused_computation.4 | loop fusion | flops 131072 | bytes 1048576 | tf_op jit(solution)/shard_map/concatenate | solution.py:373
  15.3 0.0 copy-done.4
  15.3 8.0 %all-to-all-done = bf16[32,40,128]{2,1,0:T(8,128)(2,1)S(1)} async-done(((bf16[32,40,128]{2,1,0:T(8,128)(2,1)}), bf16[32,40,128]{2,1,0:T(8,128)(2,1)S(1)}, u32[]{:S(2)}, u32[]{:S(2)}) %all-to-all-start) | async-done | bytes 327712 | tf_op jit(solution)/shard_map/all_to_all | solution.py:354
  23.4 0.7 reshape.80.meta_ref
  24.1 0.7 slice.11
  24.8 0.0 copy-start.2
  24.8 42.8 %farm.1 = bf16[1024,128]{1,0:T(8,128)(2,1)} custom-call(s32[1,2]{1,0:T(1,128)} %add_convert_fusion.flag_ref, f32[8,1024]{1,0:T(8,128)} %reshape.80.meta_ref, bf16[1024,128]{1,0:T(8,128)(2,1)} %bitcast.34, bf16[128,128]{1,0:T(8,128)(2,1)} %bitcast.36, f32[64,8,256]{2,1,0:T(8,128)} %pad_maximum_fusion.tx_ref, bf16[512,256]{1,0:T(8,128)(2,1)} %constant.108.clone.uh_ref, ...), custom_call_target="tpu_custom_call" | custom-call | tf_op jit(solution)/shard_map/farm/pallas_call | solution.py:415
  67.6 0.0 copy-start.1
  67.6 0.0 copy-start.5
  67.7 2.7 %all-to-all-start.1 = ((bf16[32,32,128]{2,1,0:T(8,128)(2,1)}), bf16[32,32,128]{2,1,0:T(8,128)(2,1)S(1)}, u32[]{:S(2)}, u32[]{:S(2)}) async-start(bf16[32,32,128]{2,1,0:T(8,128)(2,1)} %bitcast.33), calls=%async_computation.1 | async-start | bytes 524288 | tf_op jit(solution)/shard_map/all_to_all | solution.py:416
  70.4 0.0 copy-done.2
  70.4 0.0 copy-done.3
  70.4 0.1 fusion.13
  70.5 0.6 gather_fusion
  71.1 0.0 copy-done
  71.1 1.2 %fusion.6 = f32[64,1,128]{2,1,0:T(1,128)S(1)} fusion(bf16[64,128,128]{2,1,0:T(8,128)(2,1)S(1)} %copy-done, bf16[64,128,1]{1,0,2:T(8,128)(2,1)S(1)} %bitcast.35), kind=kOutput, calls=%fused_computation.17 | convolution fusion | flops 2097152 | bytes 2146304 | tf_op jit(solution)/shard_map/tpq,tq->tp/dot_general | solution.py:421
  72.3 8.7 %all-to-all-done.1 = bf16[32,32,128]{2,1,0:T(8,128)(2,1)S(1)} async-done(((bf16[32,32,128]{2,1,0:T(8,128)(2,1)}), bf16[32,32,128]{2,1,0:T(8,128)(2,1)S(1)}, u32[]{:S(2)}, u32[]{:S(2)}) %all-to-all-start.1) | async-done | bytes 262176 | tf_op jit(solution)/shard_map/all_to_all | solution.py:416
  81.0 0.1 reduce_sum.12
  81.0 0.0 copy-done.1
  81.1 0.6 fusion.8
  81.7 0.0 copy-done.5
  81.7 0.9 %fusion.1 = bf16[32,128]{1,0:T(8,128)(2,1)} fusion(f32[32,128]{1,0:T(8,128)S(1)} %bitcast.40, f32[64,128]{1,0:T(8,128)S(1)} %bitcast.39, s32[64]{0:T(128)S(1)} %copy-done.5, s32[32]{0:T(128)S(1)} %copy-done.3), kind=kOutput, calls=%fused_computation.3 | convolution fusion | flops 3164160 | bytes 57728 | tf_op jit(solution)/shard_map/tb,tp->bp/dot_general | solution.py:423
  (10 shorter events, 0.1 us)
Async XLA Ops:
  0.0 71.1 %copy-start = (bf16[64,128,128]{2,1,0:T(8,128)(2,1)S(1)}, bf16[64,128,128]{2,1,0:T(8,128)(2,1)}, u32[]{:S(2)}) copy-start(bf16[64,128,128]{2,1,0:T(8,128)(2,1)} %param.22) | copy-start | bytes 6291460
  0.0 15.3 %copy-start.4 = (s32[64]{0:T(128)S(1)}, s32[64]{0:T(128)}, u32[]{:S(2)}) copy-start(s32[64]{0:T(128)} %param.21) | copy-start | bytes 772
  4.1 19.3 %all-to-all-start = ((bf16[32,40,128]{2,1,0:T(8,128)(2,1)}), bf16[32,40,128]{2,1,0:T(8,128)(2,1)S(1)}, u32[]{:S(2)}, u32[]{:S(2)}) async-start(bf16[32,40,128]{2,1,0:T(8,128)(2,1)} %broadcast_in_dim.9), calls=%async_computation | async-start | bytes 655360 | tf_op jit(solution)/shard_map/all_to_all | solution.py:354
  24.8 45.6 %copy-start.2 = (bf16[32,128]{1,0:T(8,128)(2,1)S(1)}, bf16[32,128]{1,0:T(8,128)(2,1)}, u32[]{:S(2)}) copy-start(bf16[32,128]{1,0:T(8,128)(2,1)} %param.15) | copy-start | bytes 24580
  24.8 45.6 %copy-start.3 = (s32[32]{0:T(128)S(1)}, s32[32]{0:T(128)}, u32[]{:S(2)}) copy-start(s32[32]{0:T(128)} %param.16) | copy-start | bytes 388
  67.6 13.4 %copy-start.1 = (bf16[32,128,128]{2,1,0:T(8,128)(2,1)S(1)}, bf16[32,128,128]{2,1,0:T(8,128)(2,1)}, u32[]{:S(2)}) copy-start(bf16[32,128,128]{2,1,0:T(8,128)(2,1)} %param.17) | copy-start | bytes 3145732
  67.6 14.0 %copy-start.5 = (s32[64]{0:T(128)S(1)}, s32[64]{0:T(128)}, u32[]{:S(2)}) copy-start(s32[64]{0:T(128)} %param.20) | copy-start | bytes 772
  67.7 13.3 %all-to-all-start.1 = ((bf16[32,32,128]{2,1,0:T(8,128)(2,1)}), bf16[32,32,128]{2,1,0:T(8,128)(2,1)S(1)}, u32[]{:S(2)}, u32[]{:S(2)}) async-start(bf16[32,32,128]{2,1,0:T(8,128)(2,1)} %bitcast.33), calls=%async_computation.1 | async-start | bytes 524288 | tf_op jit(solution)/shard_map/all_to_all | solution.py:416

commit v4 on v3

--- a/solution.py
+++ b/solution.py
@@ -14,6 +14,7 @@
 CHUNK = 32
 BOX_X = 8
 LANES = CHUNK * BOX_X
+UNROLL = 4
 TILE = 8
 SLOTS = TILE * CHUNK
 f32 = jnp.float32
@@ -79,10 +80,32 @@
     return jnp.where(mask, 1.0, 0.0).astype(bf16)
 
 
+def pack_kernel(grid_shape, charge_ref, live_ref, weight_ref, slab_ref, index_ref, out_ref, packet_ref):
+    slab_boxes, row_boxes, x_boxes = grid_shape
+    blocks, slots = charge_ref.shape
+    counts = jnp.where(iota((blocks, blocks), 0) == iota((blocks, blocks), 1), live_ref[...], 0)
+    live = iota((blocks, slots), 1) < jnp.sum(counts, axis=1, keepdims=True)
+    charge = jnp.where(live, charge_ref[...].astype(f32), 0.0).astype(bf16)
+    for b in range(blocks):
+        packet_ref[b : b + 1, :] = dot(charge, weight_ref[b])[b : b + 1]
+    packet_ref[blocks : blocks + 8, :] = jnp.zeros((8, slots), f32)
+    place, x = index_ref[...] // x_boxes, index_ref[...] % x_boxes
+    box = (slab_ref[...] * slab_boxes + place // row_boxes, place % row_boxes, x)
+    for n in range(3):
+        packet_ref[blocks + n : blocks + n + 1, 0:blocks] = box[n].astype(f32)
+    packet = packet_ref[...].astype(bf16)
+
+    def copy(d, carry):
+        out_ref[d] = packet
+        return carry
+
+    lax.fori_loop(0, out_ref.shape[0], copy, 0)
+
+
 def farm_kernel(
-    keep, half, flag_ref, meta_ref, rows_ref, ty_ref, tx_ref, uh_ref, ul_ref, ih_ref, il_ref, kernel_ref,
+    keep, half, pens, flag_ref, packets_ref, ty_ref, tx_ref, uh_ref, ul_ref, ih_ref, il_ref, kernel_ref,
     out_ref, grid_ref, cols_ref, edge_ref, ex_ref, eh_ref, el_ref, along_ref, kh_ref, sx_ref, yl_ref, got_ref, acc_ref,
-    place_ref, boxes_ref, index_ref, cz_ref, xb_ref, kernel_sems, index_sems,
+    meta_ref, rows_ref, place_ref, boxes_ref, index_ref, cz_ref, xb_ref, kernel_sems, index_sems,
 ):
     depth, cv, _ = grid_ref.shape
     z_boxes = depth // 4
@@ -101,6 +124,21 @@
     for copy in copies:
         copy.start()
 
+    own = packets_ref.shape[1] - 8
+
+    def unpack(g, carry):
+        meta = jnp.zeros((8, 128), f32)
+        for n in range(128 // own):
+            d = 128 // own * g + n
+            rows_ref[pl.ds(pl.multiple_of(own * d, own), own), :] = packets_ref[d, 0:own, :]
+            shift = n % pens * (y_boxes // pens)
+            shifted = (iota((8, 128), 0) == 1) & (iota((8, 128), 1) < own)
+            part = packets_ref[d, own : own + 8, :].astype(f32) + jnp.where(shifted, float(shift), 0.0)
+            meta = meta + (pltpu.roll(part, own * n, 1) if n else part)
+        meta_ref[:, pl.ds(pl.multiple_of(128 * g, 128), 128)] = meta
+        return carry
+
+    lax.fori_loop(0, groups, unpack, 0)
     below = ones_where(iota((128, 128), 0) < iota((128, 128), 1))
     base = jnp.zeros((z_boxes, 128), f32)
     marks, before = [], []
@@ -125,8 +163,8 @@
     copy = pltpu.make_async_copy(boxes_ref, cz_ref, index_sems.at[0])
     copy.start()
     copy.wait()
-    steps = (cz_ref[1, 0] + 1) // 2
-    tiles = (2 * steps + TILE - 1) // TILE
+    steps = (cz_ref[1, 0] + (UNROLL - 1)) // UNROLL
+    tiles = (UNROLL * steps + TILE - 1) // TILE
     row, col = iota((LANES, LANES), 0), iota((LANES, LANES), 1)
     to_lanes = ones_where((row // CHUNK == col % BOX_X) & (row % CHUNK == col // BOX_X))
     from_lanes = ones_where((col // CHUNK == row % BOX_X) & (col % CHUNK == row // BOX_X))
@@ -173,8 +211,8 @@
         return jnp.minimum(cz_ref[0, c], depth // 4 - 1)
 
     def scatter(step, carry):
-        for n in range(2):
-            c = 2 * step + n
+        for n in range(UNROLL):
+            c = UNROLL * step + n
             (ex_high, ex_low), along = tables(c, n)
             if keep:
                 eh_ref[c], el_ref[c], along_ref[c] = ex_high, ex_low, along
@@ -189,7 +227,7 @@
                 edges.append((line[0] - line[1]) + (line[2] - line[3]))
             edges.append(jnp.zeros((4, LANES), f32))
             high, low = split(jnp.concatenate(parts + edges, axis=0))
-            added = stacked(dot, high, low, ex_high, ex_low)
+            added = dot3(high, low, ex_high, ex_low)
             where = pl.ds(4 * box_of(c), 4)
             grid_ref[where] = grid_ref[where] + added[: 4 * cv].reshape(4, cv, 2 * nw)
             edge_ref[box_of(c)] = edge_ref[box_of(c)] + added[4 * cv :]
@@ -218,8 +256,10 @@
         back = dot3(ih_ref[...], il_ref[...], high, low)
         return back[:depth], back[depth:]
 
+    pairs = min(4, nv // 2)
+
     def column(step, carry):
-        for p in (2 * step, 2 * step + 1):
+        for p in [pairs * step + n for n in range(pairs)]:
             real, imag = [], []
             for v in (2 * p, 2 * p + 1):
                 re, im = cols_ref[v], cols_ref[nv + v]
@@ -234,7 +274,7 @@
 
     for copy in copies:
         copy.wait()
-    lax.fori_loop(0, nv // 4, column, 0)
+    lax.fori_loop(0, nv // 2 // pairs, column, 0)
 
     edge = jnp.concatenate([edge_ref[z][0:4] for z in range(depth // 4)], axis=0)
     q_re, q_im = filtered([edge[:, :nw]], [edge[:, nw:]], (nv,))
@@ -252,8 +292,8 @@
     lax.fori_loop(0, cv // 8, to_planes, 0)
 
     def gather(step, carry):
-        for n in range(2):
-            c = 2 * step + n
+        for n in range(UNROLL):
+            c = UNROLL * step + n
             if keep:
                 ex_high, ex_low, along = eh_ref[c], el_ref[c], along_ref[c]
             else:
@@ -284,7 +324,7 @@
         got_ref[c] = jnp.zeros((16, LANES), bf16)
         return carry
 
-    lax.fori_loop(2 * steps, TILE * tiles, wipe, 0)
+    lax.fori_loop(UNROLL * steps, TILE * tiles, wipe, 0)
 
     def unsort(t, carry):
         lines = got_ref[pl.ds(TILE * t, TILE)].reshape(TILE * 16, LANES)
@@ -342,18 +382,18 @@
 
     live = jnp.arange(slots, dtype=jnp.int32)[None, :] < counts[:, None]
     charge = jnp.where(live, charges, jnp.zeros_like(charges))
-    spread = jnp.einsum("bp,bps->bs", charge, proj_weight, preferred_element_type=f32)
-
-    per_plane = rows_pen // 4 * x_boxes
-    box_z = dest_slab[:, 0] * (planes // 4) + box_index // per_plane
-    box_y = pen * (rows_pen // 4) + box_index // x_boxes % (rows_pen // 4)
-    box_x = box_index % x_boxes
-    meta = jnp.stack([box_z, box_y, box_x]).astype(bf16)
-    meta = jnp.pad(meta, ((0, 5), (0, stencil - blocks)))
-    packet = jnp.concatenate([spread.astype(bf16), meta], axis=0)
-    packets = lax.all_to_all(jnp.broadcast_to(packet, (devices,) + packet.shape), AXES, 0, 0, tiled=True)
-    rows = packets[:, :blocks].reshape(total_blocks, stencil)
-    boxes = packets[:, blocks:, :blocks].transpose(1, 0, 2).reshape(8, total_blocks).astype(f32)
+    vmem = pl.BlockSpec(memory_space=pltpu.VMEM)
+    smem = pl.BlockSpec(memory_space=pltpu.SMEM)
+    pack = pl.pallas_call(
+        functools.partial(pack_kernel, (planes // 4, rows_pen // 4, x_boxes)),
+        out_shape=jax.ShapeDtypeStruct((devices, blocks + 8, stencil), bf16),
+        scratch_shapes=[pltpu.VMEM((blocks + 8, stencil), f32)],
+        in_specs=[vmem] * 5,
+        out_specs=vmem,
+        name="pack",
+    )
+    packets = pack(charges, counts[None, :], proj_weight, dest_slab.reshape(1, blocks), box_index[None, :])
+    packets = lax.all_to_all(packets, AXES, 0, 0, tiled=True)
 
     v_all, yb_all = np.arange(width_y), np.arange(y_boxes)
     cos, sin = turn(width_y, v_all[None, :, None] * (4 * yb_all[None, None, :] + np.arange(4)[:, None, None]))
@@ -380,19 +420,17 @@
     flags = jnp.stack([odd, last]).astype(jnp.int32)[None, :]
     keep = chunks <= 64
     kept = chunks if keep else 1
-    vmem = pl.BlockSpec(memory_space=pltpu.VMEM)
-    smem = pl.BlockSpec(memory_space=pltpu.SMEM)
     lane_tiles = -(-chunks // 128) * 128
     farm = pl.pallas_call(
-        functools.partial(farm_kernel, keep, half),
+        functools.partial(farm_kernel, keep, half, pen_count),
         out_shape=jax.ShapeDtypeStruct((total_blocks, stencil), bf16),
-        in_specs=[smem] + [vmem] * 8 + [pl.BlockSpec(memory_space=pl.ANY)],
+        in_specs=[smem] + [vmem] * 7 + [pl.BlockSpec(memory_space=pl.ANY)],
         out_specs=vmem,
         scratch_shapes=[
             pltpu.VMEM((depth, 2 * own, 2 * nw), f32),
             pltpu.VMEM((2 * own, depth, 2 * nw), f32),
             pltpu.VMEM((z_boxes, 8, 2 * nw), f32),
-            pltpu.VMEM((2, LANES, 2 * nw), f32),
+            pltpu.VMEM((UNROLL, LANES, 2 * nw), f32),
             pltpu.VMEM((kept, LANES, 2 * nw), bf16),
             pltpu.VMEM((kept, LANES, 2 * nw), bf16),
             pltpu.VMEM((kept, 8 * own, LANES), f32),
@@ -401,6 +439,8 @@
             pltpu.VMEM((chunks, LANES), f32),
             pltpu.VMEM((chunks, 16, LANES), bf16),
             pltpu.VMEM((stencil, total_blocks), f32),
+            pltpu.VMEM((8, total_blocks), f32),
+            pltpu.VMEM((total_blocks, stencil), bf16),
             pltpu.VMEM((1, total_blocks), jnp.int32),
             pltpu.VMEM((2, lane_tiles), jnp.int32),
             pltpu.VMEM((1, chunks * CHUNK), jnp.int32),
@@ -412,7 +452,7 @@
         compiler_params=pltpu.CompilerParams(vmem_limit_bytes=58 << 20),
         name="farm",
     )
-    partial = farm(flags, boxes, rows, ty, tx, jnp.asarray(uh), jnp.asarray(ul), jnp.asarray(ih), jnp.asarray(il), kernel_hat)
+    partial = farm(flags, packets, ty, tx, jnp.asarray(uh), jnp.asarray(ul), jnp.asarray(ih), jnp.asarray(il), kernel_hat)
     shares = lax.all_to_all(partial.reshape(devices, blocks, stencil), AXES, 0, 0, tiled=True)
     samples = jnp.sum(shares.astype(f32), axis=0).astype(bf16)
 

time: 83.4 us -> 76.2 us (0.914); the launches traced: 82.6 us -> 76.6 us
  other arithmetic: 5.74 us -> 4.11 us
  matrix products: 4.3 us -> 2.71 us
  local copies, waits for them, and re-layouts: 2.89 us -> 1.39 us
  Pallas kernels: 42.8 us -> 41.6 us
    dot_general x1 -> x0, matrix products: 1.6 us -> none  [shards(): jnp.einsum('bp,bps->bs', charge, proj_weight, preferred_element_type=f32)]
    pallas_call x1 -> x2, Pallas kernels: 42.8 us -> 41.6 us  [the longest x1 38.8 us: shards(): farm(flags, packets, ty, tx, jnp.asarray(uh), jnp.asarray(ul), jnp.asarra...]
    select_n x2 -> x1, other arithmetic: 1.01 us -> 0.07 us  [shards(): charge = jnp.where(live, charges, jnp.zeros_like(charges))]
  transfers between devices with their start and end apart: 2 -> 2, of which waited for: 2 -> 2; matrix products, arithmetic and copies ran while one was open for 7% -> 8% of each run, Pallas kernels for 0% -> 0%
where the time goes in v4:
time: 76.2 us; the launch traced here: 76.6 us
  Pallas kernels  41.6 us (55%)
  waiting for transfers between devices  16.6 us (22%)
  starting transfers between devices  10 us (13%)
  other arithmetic  4.11 us (5%)
  matrix products  2.71 us (4%)
  local copies, waits for them, and re-layouts  1.39 us (2%)
    pallas_call x1, Pallas kernels, shards(): farm(flags, packets, ty, tx, jnp.asarray(uh), jnp.asarray(ul), jnp.asarra...  38.8 us
    all_to_all x1, waiting for transfers between devices, shards(): lax.all_to_all(partial.reshape(devices, blocks, stencil), AXES, 0, 0, til...  8.67 us
    all_to_all x1, waiting for transfers between devices, shards(): packets = lax.all_to_all(packets, AXES, 0, 0, tiled=True)  7.97 us
    all_to_all x1, starting transfers between devices, shards(): packets = lax.all_to_all(packets, AXES, 0, 0, tiled=True)  7.3 us
    pallas_call x1, Pallas kernels, shards(): pack(charges, counts[None, :], proj_weight, dest_slab.reshape(1, blocks),...  2.79 us
    all_to_all x1, starting transfers between devices, shards(): lax.all_to_all(partial.reshape(devices, blocks, stencil), AXES, 0, 0, til...  2.73 us
  transfers between devices with their start and end apart: 2, of which 2 were waited for; matrix products, arithmetic and copies ran while one was open for 8% of the time, Pallas kernels for 0%

profile of v4, /device:TPU:0, one launch (start us, length us, event | category | flops | bytes accessed | tf_op | source)
XLA Modules:
  0.0 76.6 jit_solution(9695057170610462021)
XLA Ops:
  0.0 0.0 copy-start
  0.0 0.0 copy-start.5
  0.0 2.8 %pack.1 = bf16[32,40,128]{2,1,0:T(8,128)(2,1)} custom-call(bf16[32,128]{1,0:T(8,128)(2,1)} %charge_ref.1, s32[1,32]{1,0:T(1,128)} %bitcast.22, bf16[32,128,128]{2,1,0:T(8,128)(2,1)} %weight_ref.1, s32[1,32]{1,0:T(1,128)} %bitcast.23, s32[1,32]{1,0:T(1,128)} %bitcast.24), custom_call_target="tpu_custom_call" | custom-call | tf_op jit(solution)/shard_map/pack/pallas_call | solution.py:395
  2.8 7.3 %all-to-all-start = ((bf16[32,40,128]{2,1,0:T(8,128)(2,1)}), bf16[32,40,128]{2,1,0:T(8,128)(2,1)S(1)}, u32[]{:S(2)}, u32[]{:S(2)}) async-start(bf16[32,40,128]{2,1,0:T(8,128)(2,1)} %pack.1), calls=%async_computation | async-start | bytes 655360 | tf_op jit(solution)/shard_map/all_to_all | solution.py:396
  10.1 1.4 %dynamic-slice_select_fusion = bf16[4,2,16,128]{3,2,1,0:T(8,128)(2,1)} fusion(bf16[4,2,128,128]{3,2,1,0:T(8,128)(2,1)} %constant.58.clone, s32[]{:T(128)S(6)} %select_n.33, bf16[4,2,128,128]{3,2,1,0:T(8,128)(2,1)} %constant.57.clone, pred[]{:T(512)} %ge.3), kind=kLoop, calls=%fused_computation.15 | loop fusion | flops 16384 | bytes 98309 | tf_op jit(solution)/shard_map/jit(_where)/select_n | solution.py:407
  11.5 0.6 add_convert_fusion.flag_ref
  12.2 1.1 %fusion.5 = (f32[64,8,128]{2,1,0:T(8,128)S(1)}, f32[64,8,128]{2,1,0:T(8,128)S(1)}) fusion(s32[128]{0:T(128)S(1)} %iota_add_fusion, s32[64,8]{1,0:T(8,128)S(1)} %multiply_add_fusion), kind=kLoop, calls=%fused_computation.14 | loop fusion | flops 983040 | bytes 526848 | tf_op jit(solution)/shard_map/cos | solution.py:413
  13.3 0.8 %pad_maximum_fusion.tx_ref = f32[64,8,256]{2,1,0:T(8,128)} fusion(f32[64,8,128]{2,1,0:T(8,128)S(1)} %get-tuple-element.6, f32[64,8,128]{2,1,0:T(8,128)S(1)} %get-tuple-element.5), kind=kLoop, calls=%fused_computation.4 | loop fusion | flops 131072 | bytes 1048576 | tf_op jit(solution)/shard_map/concatenate | solution.py:413
  14.1 0.0 copy-done.5
  14.1 8.0 %all-to-all-done.packets_ref = bf16[32,40,128]{2,1,0:T(8,128)(2,1)S(1)} async-done(((bf16[32,40,128]{2,1,0:T(8,128)(2,1)}), bf16[32,40,128]{2,1,0:T(8,128)(2,1)S(1)}, u32[]{:S(2)}, u32[]{:S(2)}) %all-to-all-start) | async-done | bytes 327712 | tf_op jit(solution)/shard_map/all_to_all | solution.py:396
  22.1 0.0 copy-start.2
  22.1 0.7 copy-done.2
  22.8 0.0 copy-start.3
  22.8 0.0 copy-start.4
  22.8 38.8 %farm.1 = bf16[1024,128]{1,0:T(8,128)(2,1)} custom-call(s32[1,2]{1,0:T(1,128)} %add_convert_fusion.flag_ref, bf16[32,40,128]{2,1,0:T(8,128)(2,1)} %copy-done.2, bf16[128,128]{1,0:T(8,128)(2,1)} %bitcast.18, f32[64,8,256]{2,1,0:T(8,128)} %pad_maximum_fusion.tx_ref, bf16[512,256]{1,0:T(8,128)(2,1)} %constant.59.clone.uh_ref, ...), custom_call_target="tpu_custom_call" | custom-call | tf_op jit(solution)/shard_map/farm/pallas_call | solution.py:455
  61.6 0.0 copy-start.1
  61.6 0.0 copy-start.6
  61.6 2.7 %all-to-all-start.1 = ((bf16[32,32,128]{2,1,0:T(8,128)(2,1)}), bf16[32,32,128]{2,1,0:T(8,128)(2,1)S(1)}, u32[]{:S(2)}, u32[]{:S(2)}) async-start(bf16[32,32,128]{2,1,0:T(8,128)(2,1)} %bitcast.16), calls=%async_computation.1 | async-start | bytes 524288 | tf_op jit(solution)/shard_map/all_to_all | solution.py:456
  64.4 0.0 copy-done.3
  64.4 0.0 copy-done.4
  64.4 0.1 fusion.11
  64.5 0.6 gather_fusion
  65.1 0.0 copy-done
  65.1 1.2 %fusion.6 = f32[64,1,128]{2,1,0:T(1,128)S(1)} fusion(bf16[64,128,128]{2,1,0:T(8,128)(2,1)S(1)} %copy-done, bf16[64,128,1]{1,0,2:T(8,128)(2,1)S(1)} %bitcast.17), kind=kOutput, calls=%fused_computation.16 | convolution fusion | flops 2097152 | bytes 2146304 | tf_op jit(solution)/shard_map/tpq,tq->tp/dot_general | solution.py:461
  66.3 8.7 %all-to-all-done.1 = bf16[32,32,128]{2,1,0:T(8,128)(2,1)S(1)} async-done(((bf16[32,32,128]{2,1,0:T(8,128)(2,1)}), bf16[32,32,128]{2,1,0:T(8,128)(2,1)S(1)}, u32[]{:S(2)}, u32[]{:S(2)}) %all-to-all-start.1) | async-done | bytes 262176 | tf_op jit(solution)/shard_map/all_to_all | solution.py:456
  75.0 0.1 reduce_sum.12
  75.0 0.0 copy-done.1
  75.0 0.6 fusion.8
  75.7 0.0 copy-done.6
  75.7 0.9 %fusion.1 = bf16[32,128]{1,0:T(8,128)(2,1)} fusion(f32[32,128]{1,0:T(8,128)S(1)} %bitcast.21, f32[64,128]{1,0:T(8,128)S(1)} %bitcast.20, s32[64]{0:T(128)S(1)} %copy-done.6, s32[32]{0:T(128)S(1)} %copy-done.4), kind=kOutput, calls=%fused_computation.3 | convolution fusion | flops 3164160 | bytes 57728 | tf_op jit(solution)/shard_map/tb,tp->bp/dot_general | solution.py:463
  (4 shorter events, 0.0 us)
Async XLA Ops:
  0.0 65.1 %copy-start = (bf16[64,128,128]{2,1,0:T(8,128)(2,1)S(1)}, bf16[64,128,128]{2,1,0:T(8,128)(2,1)}, u32[]{:S(2)}) copy-start(bf16[64,128,128]{2,1,0:T(8,128)(2,1)} %param.22) | copy-start | bytes 6291460
  0.0 14.1 %copy-start.5 = (s32[64]{0:T(128)S(1)}, s32[64]{0:T(128)}, u32[]{:S(2)}) copy-start(s32[64]{0:T(128)} %param.21) | copy-start | bytes 772
  2.8 19.3 %all-to-all-start = ((bf16[32,40,128]{2,1,0:T(8,128)(2,1)}), bf16[32,40,128]{2,1,0:T(8,128)(2,1)S(1)}, u32[]{:S(2)}, u32[]{:S(2)}) async-start(bf16[32,40,128]{2,1,0:T(8,128)(2,1)} %pack.1), calls=%async_computation | async-start | bytes 655360 | tf_op jit(solution)/shard_map/all_to_all | solution.py:396
  22.1 0.7 copy-start.2
  22.8 41.6 %copy-start.3 = (bf16[32,128]{1,0:T(8,128)(2,1)S(1)}, bf16[32,128]{1,0:T(8,128)(2,1)}, u32[]{:S(2)}) copy-start(bf16[32,128]{1,0:T(8,128)(2,1)} %charge_ref.1) | copy-start | bytes 24580
  22.8 41.6 %copy-start.4 = (s32[32]{0:T(128)S(1)}, s32[32]{0:T(128)}, u32[]{:S(2)}) copy-start(s32[32]{0:T(128)} %param.16) | copy-start | bytes 388
  61.6 13.4 %copy-start.1 = (bf16[32,128,128]{2,1,0:T(8,128)(2,1)S(1)}, bf16[32,128,128]{2,1,0:T(8,128)(2,1)}, u32[]{:S(2)}) copy-start(bf16[32,128,128]{2,1,0:T(8,128)(2,1)} %weight_ref.1) | copy-start | bytes 3145732
  61.6 14.0 %copy-start.6 = (s32[64]{0:T(128)S(1)}, s32[64]{0:T(128)}, u32[]{:S(2)}) copy-start(s32[64]{0:T(128)} %param.20) | copy-start | bytes 772
  61.6 13.3 %all-to-all-start.1 = ((bf16[32,32,128]{2,1,0:T(8,128)(2,1)}), bf16[32,32,128]{2,1,0:T(8,128)(2,1)S(1)}, u32[]{:S(2)}, u32[]{:S(2)}) async-start(bf16[32,32,128]{2,1,0:T(8,128)(2,1)} %bitcast.16), calls=%async_computation.1 | async-start | bytes 524288 | tf_op jit(solution)/shard_map/all_to_all | solution.py:456

commit v5 on v4

--- a/solution.py
+++ b/solution.py
@@ -104,7 +104,7 @@
 
 def farm_kernel(
     keep, half, pens, flag_ref, packets_ref, ty_ref, tx_ref, uh_ref, ul_ref, ih_ref, il_ref, kernel_ref,
-    out_ref, grid_ref, cols_ref, edge_ref, ex_ref, eh_ref, el_ref, along_ref, kh_ref, sx_ref, yl_ref, got_ref, acc_ref,
+    out_ref, grid_ref, cols_ref, edge_ref, ex_ref, eh_ref, el_ref, along_ref, kh_ref, sx_ref, yl_ref, got_ref, acc_ref, hot_ref,
     meta_ref, rows_ref, place_ref, boxes_ref, index_ref, cz_ref, xb_ref, kernel_sems, index_sems,
 ):
     depth, cv, _ = grid_ref.shape
@@ -138,7 +138,7 @@
         meta_ref[:, pl.ds(pl.multiple_of(128 * g, 128), 128)] = meta
         return carry
 
-    lax.fori_loop(0, groups, unpack, 0)
+    lax.fori_loop(0, groups, unpack, 0, unroll=groups <= 8)
     below = ones_where(iota((128, 128), 0) < iota((128, 128), 1))
     base = jnp.zeros((z_boxes, 128), f32)
     marks, before = [], []
@@ -162,6 +162,13 @@
     boxes_ref[1:2, 0:128] = jnp.sum(used, axis=0, keepdims=True)
     copy = pltpu.make_async_copy(boxes_ref, cz_ref, index_sems.at[0])
     copy.start()
+
+    def clear(z, carry):
+        grid_ref[z] = jnp.zeros((cv, 2 * nw), f32)
+        return carry
+
+    lax.fori_loop(0, depth, clear, 0)
+    edge_ref[...] = jnp.zeros_like(edge_ref)
     copy.wait()
     steps = (cz_ref[1, 0] + (UNROLL - 1)) // UNROLL
     tiles = (UNROLL * steps + TILE - 1) // TILE
@@ -173,6 +180,8 @@
 
     def sort(t, carry):
         hot = ones_where(iota((SLOTS, blocks), 0) + SLOTS * t == place_ref[0:1, :])
+        if keep:
+            hot_ref[t] = hot
         ordered = dot(hot, rows_ref[...]).astype(bf16)
         turned = dot_nt(points_first, ordered)
         lines = exchanged([turned[16 * k : 16 * k + 16] for k in range(BOX_X)])
@@ -192,13 +201,6 @@
     copy = pltpu.make_async_copy(index_ref, xb_ref, index_sems.at[1])
     copy.start()
     copy.wait()
-
-    def clear(z, carry):
-        grid_ref[z] = jnp.zeros((cv, 2 * nw), f32)
-        return carry
-
-    lax.fori_loop(0, depth, clear, 0)
-    edge_ref[...] = jnp.zeros_like(edge_ref)
 
     def tables(c, n):
         for b in range(CHUNK):
@@ -330,7 +332,7 @@
         lines = got_ref[pl.ds(TILE * t, TILE)].reshape(TILE * 16, LANES)
         lines = dot(lines, from_lanes)
         rows = exchanged([lines[16 * q : 16 * q + 16] for q in range(TILE)])
-        hot = ones_where(iota((SLOTS, blocks), 0) + SLOTS * t == place_ref[0:1, :])
+        hot = hot_ref[t] if keep else ones_where(iota((SLOTS, blocks), 0) + SLOTS * t == place_ref[0:1, :])
         acc_ref[...] += dot(jnp.concatenate(rows, axis=0).astype(bf16), hot)
         return carry
 
@@ -439,6 +441,7 @@
             pltpu.VMEM((chunks, LANES), f32),
             pltpu.VMEM((chunks, 16, LANES), bf16),
             pltpu.VMEM((stencil, total_blocks), f32),
+            pltpu.VMEM((-(-kept // TILE), SLOTS, total_blocks if keep else 128), bf16),
             pltpu.VMEM((8, total_blocks), f32),
             pltpu.VMEM((total_blocks, stencil), bf16),
             pltpu.VMEM((1, total_blocks), jnp.int32),

time: 76.2 us -> 75.7 us (level)
  Pallas kernels: 41.6 us -> 40.4 us
    pallas_call x1, Pallas kernels: 38.8 us -> 37.6 us  [shards(): farm(flags, packets, ty, tx, jnp.asarray(uh), jnp.asarray(ul), jnp.asarra...]
where the time goes in v5:
time: 75.7 us; the launch traced here: 75.4 us
  Pallas kernels  40.4 us (53%)
  waiting for transfers between devices  16.6 us (22%)
  starting transfers between devices  10 us (13%)
  other arithmetic  4.11 us (5%)
  matrix products  2.71 us (4%)
  local copies, waits for them, and re-layouts  1.39 us (2%)
    pallas_call x1, Pallas kernels, shards(): farm(flags, packets, ty, tx, jnp.asarray(uh), jnp.asarray(ul), jnp.asarra...  37.6 us
    all_to_all x1, waiting for transfers between devices, shards(): lax.all_to_all(partial.reshape(devices, blocks, stencil), AXES, 0, 0, til...  8.67 us
    all_to_all x1, waiting for transfers between devices, shards(): packets = lax.all_to_all(packets, AXES, 0, 0, tiled=True)  7.97 us
    all_to_all x1, starting transfers between devices, shards(): packets = lax.all_to_all(packets, AXES, 0, 0, tiled=True)  7.3 us
    pallas_call x1, Pallas kernels, shards(): pack(charges, counts[None, :], proj_weight, dest_slab.reshape(1, blocks),...  2.79 us
    all_to_all x1, starting transfers between devices, shards(): lax.all_to_all(partial.reshape(devices, blocks, stencil), AXES, 0, 0, til...  2.73 us
  transfers between devices with their start and end apart: 2, of which 2 were waited for; matrix products, arithmetic and copies ran while one was open for 8% of the time, Pallas kernels for 0%

profile of v5, /device:TPU:0, one launch (start us, length us, event | category | flops | bytes accessed | tf_op | source)
XLA Modules:
  0.0 75.4 jit_solution(17018317512707570324)
XLA Ops:
  0.0 0.0 copy-start
  0.0 0.0 copy-start.5
  0.0 2.8 %pack.1 = bf16[32,40,128]{2,1,0:T(8,128)(2,1)} custom-call(bf16[32,128]{1,0:T(8,128)(2,1)} %charge_ref.1, s32[1,32]{1,0:T(1,128)} %bitcast.22, bf16[32,128,128]{2,1,0:T(8,128)(2,1)} %weight_ref.1, s32[1,32]{1,0:T(1,128)} %bitcast.23, s32[1,32]{1,0:T(1,128)} %bitcast.24), custom_call_target="tpu_custom_call" | custom-call | tf_op jit(solution)/shard_map/pack/pallas_call | solution.py:397
  2.8 7.3 %all-to-all-start = ((bf16[32,40,128]{2,1,0:T(8,128)(2,1)}), bf16[32,40,128]{2,1,0:T(8,128)(2,1)S(1)}, u32[]{:S(2)}, u32[]{:S(2)}) async-start(bf16[32,40,128]{2,1,0:T(8,128)(2,1)} %pack.1), calls=%async_computation | async-start | bytes 655360 | tf_op jit(solution)/shard_map/all_to_all | solution.py:398
  10.1 1.4 %dynamic-slice_select_fusion = bf16[4,2,16,128]{3,2,1,0:T(8,128)(2,1)} fusion(bf16[4,2,128,128]{3,2,1,0:T(8,128)(2,1)} %constant.58.clone, s32[]{:T(128)S(6)} %select_n.33, bf16[4,2,128,128]{3,2,1,0:T(8,128)(2,1)} %constant.57.clone, pred[]{:T(512)} %ge.3), kind=kLoop, calls=%fused_computation.15 | loop fusion | flops 16384 | bytes 98309 | tf_op jit(solution)/shard_map/jit(_where)/select_n | solution.py:409
  11.5 0.6 add_convert_fusion.flag_ref
  12.2 1.1 %fusion.5 = (f32[64,8,128]{2,1,0:T(8,128)S(1)}, f32[64,8,128]{2,1,0:T(8,128)S(1)}) fusion(s32[128]{0:T(128)S(1)} %iota_add_fusion, s32[64,8]{1,0:T(8,128)S(1)} %multiply_add_fusion), kind=kLoop, calls=%fused_computation.14 | loop fusion | flops 983040 | bytes 526848 | tf_op jit(solution)/shard_map/cos | solution.py:415
  13.3 0.8 %pad_maximum_fusion.tx_ref = f32[64,8,256]{2,1,0:T(8,128)} fusion(f32[64,8,128]{2,1,0:T(8,128)S(1)} %get-tuple-element.6, f32[64,8,128]{2,1,0:T(8,128)S(1)} %get-tuple-element.5), kind=kLoop, calls=%fused_computation.4 | loop fusion | flops 131072 | bytes 1048576 | tf_op jit(solution)/shard_map/concatenate | solution.py:415
  14.1 0.0 copy-done.5
  14.1 8.0 %all-to-all-done.packets_ref = bf16[32,40,128]{2,1,0:T(8,128)(2,1)S(1)} async-done(((bf16[32,40,128]{2,1,0:T(8,128)(2,1)}), bf16[32,40,128]{2,1,0:T(8,128)(2,1)S(1)}, u32[]{:S(2)}, u32[]{:S(2)}) %all-to-all-start) | async-done | bytes 327712 | tf_op jit(solution)/shard_map/all_to_all | solution.py:398
  22.1 0.0 copy-start.2
  22.1 0.7 copy-done.2
  22.8 0.0 copy-start.3
  22.8 0.0 copy-start.4
  22.8 37.6 %farm.1 = bf16[1024,128]{1,0:T(8,128)(2,1)} custom-call(s32[1,2]{1,0:T(1,128)} %add_convert_fusion.flag_ref, bf16[32,40,128]{2,1,0:T(8,128)(2,1)} %copy-done.2, bf16[128,128]{1,0:T(8,128)(2,1)} %bitcast.18, f32[64,8,256]{2,1,0:T(8,128)} %pad_maximum_fusion.tx_ref, bf16[512,256]{1,0:T(8,128)(2,1)} %constant.59.clone.uh_ref, ...), custom_call_target="tpu_custom_call" | custom-call | tf_op jit(solution)/shard_map/farm/pallas_call | solution.py:458
  60.5 0.0 copy-start.1
  60.5 0.0 copy-start.6
  60.5 2.7 %all-to-all-start.1 = ((bf16[32,32,128]{2,1,0:T(8,128)(2,1)}), bf16[32,32,128]{2,1,0:T(8,128)(2,1)S(1)}, u32[]{:S(2)}, u32[]{:S(2)}) async-start(bf16[32,32,128]{2,1,0:T(8,128)(2,1)} %bitcast.16), calls=%async_computation.1 | async-start | bytes 524288 | tf_op jit(solution)/shard_map/all_to_all | solution.py:459
  63.2 0.0 copy-done.3
  63.3 0.0 copy-done.4
  63.3 0.1 fusion.11
  63.3 0.6 gather_fusion
  64.0 0.0 copy-done
  64.0 1.2 %fusion.6 = f32[64,1,128]{2,1,0:T(1,128)S(1)} fusion(bf16[64,128,128]{2,1,0:T(8,128)(2,1)S(1)} %copy-done, bf16[64,128,1]{1,0,2:T(8,128)(2,1)S(1)} %bitcast.17), kind=kOutput, calls=%fused_computation.16 | convolution fusion | flops 2097152 | bytes 2146304 | tf_op jit(solution)/shard_map/tpq,tq->tp/dot_general | solution.py:464
  65.2 8.7 %all-to-all-done.1 = bf16[32,32,128]{2,1,0:T(8,128)(2,1)S(1)} async-done(((bf16[32,32,128]{2,1,0:T(8,128)(2,1)}), bf16[32,32,128]{2,1,0:T(8,128)(2,1)S(1)}, u32[]{:S(2)}, u32[]{:S(2)}) %all-to-all-start.1) | async-done | bytes 262176 | tf_op jit(solution)/shard_map/all_to_all | solution.py:459
  73.8 0.1 reduce_sum.12
  73.9 0.0 copy-done.1
  73.9 0.6 fusion.8
  74.5 0.0 copy-done.6
  74.5 0.9 %fusion.1 = bf16[32,128]{1,0:T(8,128)(2,1)} fusion(f32[32,128]{1,0:T(8,128)S(1)} %bitcast.21, f32[64,128]{1,0:T(8,128)S(1)} %bitcast.20, s32[64]{0:T(128)S(1)} %copy-done.6, s32[32]{0:T(128)S(1)} %copy-done.4), kind=kOutput, calls=%fused_computation.3 | convolution fusion | flops 3164160 | bytes 57728 | tf_op jit(solution)/shard_map/tb,tp->bp/dot_general | solution.py:466
  (4 shorter events, 0.0 us)
Async XLA Ops:
  0.0 64.0 %copy-start = (bf16[64,128,128]{2,1,0:T(8,128)(2,1)S(1)}, bf16[64,128,128]{2,1,0:T(8,128)(2,1)}, u32[]{:S(2)}) copy-start(bf16[64,128,128]{2,1,0:T(8,128)(2,1)} %param.22) | copy-start | bytes 6291460
  0.0 14.1 %copy-start.5 = (s32[64]{0:T(128)S(1)}, s32[64]{0:T(128)}, u32[]{:S(2)}) copy-start(s32[64]{0:T(128)} %param.21) | copy-start | bytes 772
  2.8 19.3 %all-to-all-start = ((bf16[32,40,128]{2,1,0:T(8,128)(2,1)}), bf16[32,40,128]{2,1,0:T(8,128)(2,1)S(1)}, u32[]{:S(2)}, u32[]{:S(2)}) async-start(bf16[32,40,128]{2,1,0:T(8,128)(2,1)} %pack.1), calls=%async_computation | async-start | bytes 655360 | tf_op jit(solution)/shard_map/all_to_all | solution.py:398
  22.1 0.7 copy-start.2
  22.8 40.4 %copy-start.3 = (bf16[32,128]{1,0:T(8,128)(2,1)S(1)}, bf16[32,128]{1,0:T(8,128)(2,1)}, u32[]{:S(2)}) copy-start(bf16[32,128]{1,0:T(8,128)(2,1)} %charge_ref.1) | copy-start | bytes 24580
  22.8 40.4 %copy-start.4 = (s32[32]{0:T(128)S(1)}, s32[32]{0:T(128)}, u32[]{:S(2)}) copy-start(s32[32]{0:T(128)} %param.16) | copy-start | bytes 388
  60.5 13.4 %copy-start.1 = (bf16[32,128,128]{2,1,0:T(8,128)(2,1)S(1)}, bf16[32,128,128]{2,1,0:T(8,128)(2,1)}, u32[]{:S(2)}) copy-start(bf16[32,128,128]{2,1,0:T(8,128)(2,1)} %weight_ref.1) | copy-start | bytes 3145732
  60.5 14.0 %copy-start.6 = (s32[64]{0:T(128)S(1)}, s32[64]{0:T(128)}, u32[]{:S(2)}) copy-start(s32[64]{0:T(128)} %param.20) | copy-start | bytes 772
  60.5 13.3 %all-to-all-start.1 = ((bf16[32,32,128]{2,1,0:T(8,128)(2,1)}), bf16[32,32,128]{2,1,0:T(8,128)(2,1)S(1)}, u32[]{:S(2)}, u32[]{:S(2)}) async-start(bf16[32,32,128]{2,1,0:T(8,128)(2,1)} %bitcast.16), calls=%async_computation.1 | async-start | bytes 524288 | tf_op jit(solution)/shard_map/all_to_all | solution.py:459

commit v6 on v5

--- a/solution.py
+++ b/solution.py
@@ -258,7 +258,7 @@
         back = dot3(ih_ref[...], il_ref[...], high, low)
         return back[:depth], back[depth:]
 
-    pairs = min(4, nv // 2)
+    pairs = min(8, nv // 2)
 
     def column(step, carry):
         for p in [pairs * step + n for n in range(pairs)]:

time: 75.7 us -> 73.7 us (0.974)
  Pallas kernels: 40.4 us -> 39.1 us
    pallas_call x1, Pallas kernels: 37.6 us -> 36.3 us  [shards(): farm(flags, packets, ty, tx, jnp.asarray(uh), jnp.asarray(ul), jnp.asarra...]
where the time goes in v6:
time: 73.7 us; the launch traced here: 74.1 us
  Pallas kernels  39.1 us (53%)
  waiting for transfers between devices  16.6 us (23%)
  starting transfers between devices  10 us (14%)
  other arithmetic  4.11 us (6%)
  matrix products  2.71 us (4%)
  local copies, waits for them, and re-layouts  1.39 us (2%)
    pallas_call x1, Pallas kernels, shards(): farm(flags, packets, ty, tx, jnp.asarray(uh), jnp.asarray(ul), jnp.asarra...  36.3 us
    all_to_all x1, waiting for transfers between devices, shards(): lax.all_to_all(partial.reshape(devices, blocks, stencil), AXES, 0, 0, til...  8.67 us
    all_to_all x1, waiting for transfers between devices, shards(): packets = lax.all_to_all(packets, AXES, 0, 0, tiled=True)  7.97 us
    all_to_all x1, starting transfers between devices, shards(): packets = lax.all_to_all(packets, AXES, 0, 0, tiled=True)  7.3 us
    pallas_call x1, Pallas kernels, shards(): pack(charges, counts[None, :], proj_weight, dest_slab.reshape(1, blocks),...  2.79 us
    all_to_all x1, starting transfers between devices, shards(): lax.all_to_all(partial.reshape(devices, blocks, stencil), AXES, 0, 0, til...  2.73 us
  transfers between devices with their start and end apart: 2, of which 2 were waited for; matrix products, arithmetic and copies ran while one was open for 8% of the time, Pallas kernels for 0%

profile of v6, /device:TPU:0, one launch (start us, length us, event | category | flops | bytes accessed | tf_op | source)
XLA Modules:
  0.0 74.1 jit_solution(1141730006177000391)
XLA Ops:
  0.0 0.0 copy-start
  0.0 0.0 copy-start.5
  0.0 2.8 %pack.1 = bf16[32,40,128]{2,1,0:T(8,128)(2,1)} custom-call(bf16[32,128]{1,0:T(8,128)(2,1)} %charge_ref.1, s32[1,32]{1,0:T(1,128)} %bitcast.22, bf16[32,128,128]{2,1,0:T(8,128)(2,1)} %weight_ref.1, s32[1,32]{1,0:T(1,128)} %bitcast.23, s32[1,32]{1,0:T(1,128)} %bitcast.24), custom_call_target="tpu_custom_call" | custom-call | tf_op jit(solution)/shard_map/pack/pallas_call | solution.py:397
  2.8 7.3 %all-to-all-start = ((bf16[32,40,128]{2,1,0:T(8,128)(2,1)}), bf16[32,40,128]{2,1,0:T(8,128)(2,1)S(1)}, u32[]{:S(2)}, u32[]{:S(2)}) async-start(bf16[32,40,128]{2,1,0:T(8,128)(2,1)} %pack.1), calls=%async_computation | async-start | bytes 655360 | tf_op jit(solution)/shard_map/all_to_all | solution.py:398
  10.1 1.4 %dynamic-slice_select_fusion = bf16[4,2,16,128]{3,2,1,0:T(8,128)(2,1)} fusion(bf16[4,2,128,128]{3,2,1,0:T(8,128)(2,1)} %constant.58.clone, s32[]{:T(128)S(6)} %select_n.33, bf16[4,2,128,128]{3,2,1,0:T(8,128)(2,1)} %constant.57.clone, pred[]{:T(512)} %ge.3), kind=kLoop, calls=%fused_computation.15 | loop fusion | flops 16384 | bytes 98309 | tf_op jit(solution)/shard_map/jit(_where)/select_n | solution.py:409
  11.5 0.6 add_convert_fusion.flag_ref
  12.2 1.1 %fusion.5 = (f32[64,8,128]{2,1,0:T(8,128)S(1)}, f32[64,8,128]{2,1,0:T(8,128)S(1)}) fusion(s32[128]{0:T(128)S(1)} %iota_add_fusion, s32[64,8]{1,0:T(8,128)S(1)} %multiply_add_fusion), kind=kLoop, calls=%fused_computation.14 | loop fusion | flops 983040 | bytes 526848 | tf_op jit(solution)/shard_map/cos | solution.py:415
  13.3 0.8 %pad_maximum_fusion.tx_ref = f32[64,8,256]{2,1,0:T(8,128)} fusion(f32[64,8,128]{2,1,0:T(8,128)S(1)} %get-tuple-element.6, f32[64,8,128]{2,1,0:T(8,128)S(1)} %get-tuple-element.5), kind=kLoop, calls=%fused_computation.4 | loop fusion | flops 131072 | bytes 1048576 | tf_op jit(solution)/shard_map/concatenate | solution.py:415
  14.1 0.0 copy-done.5
  14.1 8.0 %all-to-all-done.packets_ref = bf16[32,40,128]{2,1,0:T(8,128)(2,1)S(1)} async-done(((bf16[32,40,128]{2,1,0:T(8,128)(2,1)}), bf16[32,40,128]{2,1,0:T(8,128)(2,1)S(1)}, u32[]{:S(2)}, u32[]{:S(2)}) %all-to-all-start) | async-done | bytes 327712 | tf_op jit(solution)/shard_map/all_to_all | solution.py:398
  22.1 0.0 copy-start.2
  22.1 0.7 copy-done.2
  22.8 0.0 copy-start.3
  22.8 0.0 copy-start.4
  22.8 36.3 %farm.1 = bf16[1024,128]{1,0:T(8,128)(2,1)} custom-call(s32[1,2]{1,0:T(1,128)} %add_convert_fusion.flag_ref, bf16[32,40,128]{2,1,0:T(8,128)(2,1)} %copy-done.2, bf16[128,128]{1,0:T(8,128)(2,1)} %bitcast.18, f32[64,8,256]{2,1,0:T(8,128)} %pad_maximum_fusion.tx_ref, bf16[512,256]{1,0:T(8,128)(2,1)} %constant.59.clone.uh_ref, ...), custom_call_target="tpu_custom_call" | custom-call | tf_op jit(solution)/shard_map/farm/pallas_call | solution.py:458
  59.2 0.0 copy-start.1
  59.2 0.0 copy-start.6
  59.2 2.7 %all-to-all-start.1 = ((bf16[32,32,128]{2,1,0:T(8,128)(2,1)}), bf16[32,32,128]{2,1,0:T(8,128)(2,1)S(1)}, u32[]{:S(2)}, u32[]{:S(2)}) async-start(bf16[32,32,128]{2,1,0:T(8,128)(2,1)} %bitcast.16), calls=%async_computation.1 | async-start | bytes 524288 | tf_op jit(solution)/shard_map/all_to_all | solution.py:459
  62.0 0.0 copy-done.3
  62.0 0.0 copy-done.4
  62.0 0.1 fusion.11
  62.0 0.6 gather_fusion
  62.7 0.0 copy-done
  62.7 1.2 %fusion.6 = f32[64,1,128]{2,1,0:T(1,128)S(1)} fusion(bf16[64,128,128]{2,1,0:T(8,128)(2,1)S(1)} %copy-done, bf16[64,128,1]{1,0,2:T(8,128)(2,1)S(1)} %bitcast.17), kind=kOutput, calls=%fused_computation.16 | convolution fusion | flops 2097152 | bytes 2146304 | tf_op jit(solution)/shard_map/tpq,tq->tp/dot_general | solution.py:464
  63.9 8.7 %all-to-all-done.1 = bf16[32,32,128]{2,1,0:T(8,128)(2,1)S(1)} async-done(((bf16[32,32,128]{2,1,0:T(8,128)(2,1)}), bf16[32,32,128]{2,1,0:T(8,128)(2,1)S(1)}, u32[]{:S(2)}, u32[]{:S(2)}) %all-to-all-start.1) | async-done | bytes 262176 | tf_op jit(solution)/shard_map/all_to_all | solution.py:459
  72.5 0.1 reduce_sum.12
  72.6 0.0 copy-done.1
  72.6 0.6 fusion.8
  73.2 0.0 copy-done.6
  73.2 0.9 %fusion.1 = bf16[32,128]{1,0:T(8,128)(2,1)} fusion(f32[32,128]{1,0:T(8,128)S(1)} %bitcast.21, f32[64,128]{1,0:T(8,128)S(1)} %bitcast.20, s32[64]{0:T(128)S(1)} %copy-done.6, s32[32]{0:T(128)S(1)} %copy-done.4), kind=kOutput, calls=%fused_computation.3 | convolution fusion | flops 3164160 | bytes 57728 | tf_op jit(solution)/shard_map/tb,tp->bp/dot_general | solution.py:466
  (4 shorter events, 0.0 us)
Async XLA Ops:
  0.0 62.7 %copy-start = (bf16[64,128,128]{2,1,0:T(8,128)(2,1)S(1)}, bf16[64,128,128]{2,1,0:T(8,128)(2,1)}, u32[]{:S(2)}) copy-start(bf16[64,128,128]{2,1,0:T(8,128)(2,1)} %param.22) | copy-start | bytes 6291460
  0.0 14.1 %copy-start.5 = (s32[64]{0:T(128)S(1)}, s32[64]{0:T(128)}, u32[]{:S(2)}) copy-start(s32[64]{0:T(128)} %param.21) | copy-start | bytes 772
  2.8 19.3 %all-to-all-start = ((bf16[32,40,128]{2,1,0:T(8,128)(2,1)}), bf16[32,40,128]{2,1,0:T(8,128)(2,1)S(1)}, u32[]{:S(2)}, u32[]{:S(2)}) async-start(bf16[32,40,128]{2,1,0:T(8,128)(2,1)} %pack.1), calls=%async_computation | async-start | bytes 655360 | tf_op jit(solution)/shard_map/all_to_all | solution.py:398
  22.1 0.7 copy-start.2
  22.8 39.1 %copy-start.3 = (bf16[32,128]{1,0:T(8,128)(2,1)S(1)}, bf16[32,128]{1,0:T(8,128)(2,1)}, u32[]{:S(2)}) copy-start(bf16[32,128]{1,0:T(8,128)(2,1)} %charge_ref.1) | copy-start | bytes 24580
  22.8 39.1 %copy-start.4 = (s32[32]{0:T(128)S(1)}, s32[32]{0:T(128)}, u32[]{:S(2)}) copy-start(s32[32]{0:T(128)} %param.16) | copy-start | bytes 388
  59.2 13.4 %copy-start.1 = (bf16[32,128,128]{2,1,0:T(8,128)(2,1)S(1)}, bf16[32,128,128]{2,1,0:T(8,128)(2,1)}, u32[]{:S(2)}) copy-start(bf16[32,128,128]{2,1,0:T(8,128)(2,1)} %weight_ref.1) | copy-start | bytes 3145732
  59.2 14.0 %copy-start.6 = (s32[64]{0:T(128)S(1)}, s32[64]{0:T(128)}, u32[]{:S(2)}) copy-start(s32[64]{0:T(128)} %param.20) | copy-start | bytes 772
  59.2 13.3 %all-to-all-start.1 = ((bf16[32,32,128]{2,1,0:T(8,128)(2,1)}), bf16[32,32,128]{2,1,0:T(8,128)(2,1)S(1)}, u32[]{:S(2)}, u32[]{:S(2)}) async-start(bf16[32,32,128]{2,1,0:T(8,128)(2,1)} %bitcast.16), calls=%async_computation.1 | async-start | bytes 524288 | tf_op jit(solution)/shard_map/all_to_all | solution.py:459
